TPU v7x, 32 devices: a whole 2x2x4 slice. The times are simulated.
32 devices in a mesh: section: 4 (over y, x), coil: 4 (over z), cuts: 2 (over core).
Axes of the slice: x: 2, y: 2, z: 4, core: 2. Of those that a mesh axis runs over, the one named last changes fastest.
Arguments:
- initial: bfloat16 [2, 32, 80, 2, 128], P(None, 'coil', 'cuts'), may hold values from -6 to 6
- sens: bfloat16 [2, 8, 32, 80, 2, 128], P(None, ('coil', 'cuts')), may hold values from -2.5 to 2.5
- kspace: bfloat16 [2, 8, 32, 80, 2, 128], P(None, ('coil', 'cuts')), may hold values from -6 to 6
- mask: int32 [2, 80, 128], replicated, may hold values 0 or 1
- step_sizes: float32 [4], P('section'), may hold values from 0.3 to 1.5
- conv_in: bfloat16 [4, 128, 18], P('section'), may hold values from -1.5 to 1.5
- bias_in: float32 [4, 128], P('section'), may hold values from -3 to 3
- conv_out: bfloat16 [4, 18, 128], P('section'), may hold values from -0.1875 to 0.1875
Outputs:
- cascade_images: bfloat16 [4, 2, 32, 80, 2, 128], P('section', None, 'coil', 'cuts')
Inputs may be any that keep to these rules, and one draw needn't show every extreme that they name: `mask`: 1 marks a sampled phase-encoding line of the slab, 0 one that was not measured.
All inputs are finite; a program needn't handle non-finite values.
Results may differ from a plain program's by a relative error of at most 0.028.
Values may be sent and summed in bfloat16 or wider, within the bound.
No kernel may reach another device: no remote copies, remote signals or barrier semaphores. Data moves between devices by JAX's collectives and lax.ppermute only.
A program may use at most 128 MiB of HBM per device.

v0:
```python
import math
import jax
import jax.numpy as jnp
from jax import lax
from jax.sharding import PartitionSpec as P


def extended_2(x, sides, width):
    for axis, dim in sides:
        size, length = (lax.axis_size(axis), x.shape[dim])
        up = [(i, (i + 1) % size) for i in range(size - 1)]
        down = [(j, i) for i, j in up]
        last = lax.slice_in_dim(x, length - width, length, axis=dim)
        leading = lax.slice_in_dim(x, 0, width, axis=dim)
        before = lax.ppermute(last, axis, up)
        after = lax.ppermute(leading, axis, down)
        x = jnp.concatenate([before, x, after], axis=dim)
    return x


def from_partner(block, axis, bit):
    count = lax.axis_size(axis)
    route = []
    for low in range(count):
        high = low | 1 << bit
        if high != low and high < count:
            route += [(low, high), (high, low)]
    return lax.ppermute(block, axis, route)


def dft_table(length, sign):
    ramp = jnp.arange(length, dtype=jnp.int32)
    phase = ramp[:, None] * ramp[None, :] % length
    angle = phase.astype(jnp.float32) * (2.0 * math.pi / length)
    scale = 1.0 / math.sqrt(length)
    cosine = jnp.cos(angle) * scale
    sine = jnp.sin(angle) * (scale * sign)
    upper = jnp.concatenate([cosine, -sine], axis=1)
    lower = jnp.concatenate([sine, cosine], axis=1)
    return jnp.concatenate([upper, lower], axis=0).astype(jnp.bfloat16)


def pass_last(volume, table):
    shape = volume.shape
    flat = volume.reshape(-1, shape[-2] * shape[-1])
    return (
        jnp.dot(flat, table, preferred_element_type=jnp.float32).astype(jnp.bfloat16).reshape(shape)
    )


def pass_middle(volume, table):
    length = volume.shape[1]
    split = table.reshape(2, length, 2, length)
    return jnp.einsum("pjcz,cjdk->pkdz", volume, split, preferred_element_type=jnp.float32).astype(
        jnp.bfloat16
    )


def pass_first(volume, table):
    length = volume.shape[0]
    split = table.reshape(2, length, 2, length)
    return jnp.einsum("jycz,cjdk->kydz", volume, split, preferred_element_type=jnp.float32).astype(
        jnp.bfloat16
    )


def complex_product(sens, image):
    sens_real = sens[:, :, 0].astype(jnp.float32)
    sens_imag = sens[:, :, 1].astype(jnp.float32)
    image_real = image[:, :, 0].astype(jnp.float32)
    image_imag = image[:, :, 1].astype(jnp.float32)
    return jnp.stack(
        [
            sens_real * image_real - sens_imag * image_imag,
            sens_real * image_imag + sens_imag * image_real,
        ],
        axis=2,
    )


def conj_product(sens, back):
    sens_real = sens[:, :, 0].astype(jnp.float32)
    sens_imag = sens[:, :, 1].astype(jnp.float32)
    back_real = back[:, :, 0].astype(jnp.float32)
    back_imag = back[:, :, 1].astype(jnp.float32)
    return jnp.stack(
        [
            sens_real * back_real + sens_imag * back_imag,
            sens_real * back_imag - sens_imag * back_real,
        ],
        axis=2,
    )


def hidden_layer(extended, out_rows, weights_in, bias):
    width = extended.shape[3]
    padded = jnp.pad(extended, ((0, 0), (0, 0), (0, 0), (1, 1)))
    taps = jnp.stack(
        [
            padded[:, shift_row : shift_row + out_rows, :, shift_col : shift_col + width]
            for shift_row in range(3)
            for shift_col in range(3)
        ],
        axis=2,
    )
    taps = taps.reshape(extended.shape[0], out_rows, 18, width)
    summed = jnp.einsum("hf,xyfz->xyhz", weights_in, taps, preferred_element_type=jnp.float32)
    return jax.nn.silu(summed + bias[None, None, :, None]).astype(jnp.bfloat16)


def combine_taps(beside_all, rows):
    width = beside_all.shape[3]
    padded = jnp.pad(beside_all, ((0, 0), (0, 0), (0, 0), (1, 1)))
    total = jnp.zeros((beside_all.shape[0], rows, 2, width), jnp.float32)
    for shift_row in range(3):
        for shift_col in range(3):
            first = (3 * shift_row + shift_col) * 2
            total = (
                total
                + padded[
                    :,
                    shift_row : shift_row + rows,
                    first : first + 2,
                    shift_col : shift_col + width,
                ]
            )
    return total


def refine_rows(current, weights_in, bias, weights_out):
    rows = current.shape[1]
    extended = extended_2(current, (("cuts", 1),), 1)
    hidden = hidden_layer(extended, rows, weights_in, bias)
    product = jnp.einsum("fh,xyhz->xyfz", weights_out, hidden, preferred_element_type=jnp.float32)
    beside_all = extended_2(product.astype(jnp.bfloat16), (("cuts", 1),), 1).astype(product.dtype)
    return combine_taps(beside_all, rows)


def whole_rows(current):
    return lax.all_gather(current, "cuts", axis=1, tiled=True)


def sum_gradient(back_rows, current):
    mine = lax.psum_scatter(
        back_rows(jnp.int32(0), lax.axis_size("coil") * current.shape[0]).astype(jnp.bfloat16),
        "coil",
        scatter_dimension=0,
        tiled=True,
    )
    grad = lax.psum_scatter(mine, "cuts", scatter_dimension=1, tiled=True).astype(jnp.float32)
    return grad


def finish_step(current, grad, step, weights_in, bias, weights_out):
    refine = refine_rows(current, weights_in, bias, weights_out)
    return (current.astype(jnp.float32) - step * grad + refine).astype(jnp.bfloat16)


def pair_block(current, sens_one, data_one, mask_one, step, weights_in, bias, weights_out, half):
    halves = whole_rows(current)
    whole = lax.all_gather(halves, "coil", axis=0, tiled=True)
    size_x, size_y, _, size_z = whole.shape
    half_x = size_x // 2
    half_y = size_y // 2
    forward_x, forward_y, forward_z = (
        dft_table(size_x, 1.0),
        dft_table(size_y, 1.0),
        dft_table(size_z, 1.0),
    )
    back_x, back_y, back_z = (
        dft_table(size_x, -1.0),
        dft_table(size_y, -1.0),
        dft_table(size_z, -1.0),
    )
    lower_side = half == 0
    x_start = half * half_x
    x_other = (1 - half) * half_x
    y_start = half * half_y
    y_other = (1 - half) * half_y
    rows_in = lax.dynamic_slice_in_dim(whole, x_start, half_x, 0)
    sens_rows = lax.dynamic_slice_in_dim(sens_one, x_start, half_x, 0)
    coil_image = complex_product(sens_rows, rows_in).astype(jnp.bfloat16)
    partial_value = pass_middle(pass_last(coil_image, forward_z), forward_y)
    kept = lax.dynamic_slice_in_dim(partial_value, y_start, half_y, 1)
    sent = lax.dynamic_slice_in_dim(partial_value, y_other, half_y, 1)
    arrived = from_partner(sent, "section", 0)
    assembled = jnp.concatenate(
        [jnp.where(lower_side, kept, arrived), jnp.where(lower_side, arrived, kept)], axis=0
    )
    predicted = pass_first(assembled, forward_x)
    data_half = lax.dynamic_slice_in_dim(data_one, y_start, half_y, 1)
    mask_half = lax.dynamic_slice_in_dim(mask_one, y_start, half_y, 0)
    weight_mask = mask_half.astype(jnp.float32)[None, :, None, :]
    resid = (weight_mask * (data_half.astype(jnp.float32) - predicted.astype(jnp.float32))).astype(
        jnp.bfloat16
    )
    spectrum = pass_first(resid, back_x)
    kept_back = lax.dynamic_slice_in_dim(spectrum, x_start, half_x, 0)
    sent_back = lax.dynamic_slice_in_dim(spectrum, x_other, half_x, 0)
    arrived_back = from_partner(sent_back, "section", 0)
    joined = jnp.concatenate(
        [
            jnp.where(lower_side, kept_back, arrived_back),
            jnp.where(lower_side, arrived_back, kept_back),
        ],
        axis=1,
    )
    back = pass_last(pass_middle(joined, back_y), back_z)
    term = conj_product(sens_rows, back)
    blank = jnp.zeros_like(term)
    full_term = jnp.concatenate(
        [jnp.where(lower_side, term, blank), jnp.where(lower_side, blank, term)], axis=0
    )

    def back_rows(start, count):
        return full_term

    grad = sum_gradient(back_rows, current)
    grad = grad + from_partner(grad.astype(jnp.bfloat16), "section", 0).astype(grad.dtype)
    return finish_step(current, grad, step, weights_in, bias, weights_out)


def body(initial, sens, kspace, mask, step_sizes, conv_in, bias_in, conv_out):
    section_count = lax.axis_size("section")
    position = lax.axis_index("section")
    all_steps, all_bias = (
        lax.all_gather(step_sizes, "section", axis=0, tiled=True),
        lax.all_gather(bias_in, "section", axis=0, tiled=True),
    )
    all_in, all_out = (
        lax.all_gather(conv_in, "section", axis=0, tiled=True),
        lax.all_gather(conv_out, "section", axis=0, tiled=True),
    )
    slab = position // 2
    half = position % 2
    current = lax.dynamic_index_in_dim(initial, slab, 0, keepdims=False)
    sens_one = lax.dynamic_index_in_dim(sens, slab, 0, keepdims=False)[0]
    data_one = lax.dynamic_index_in_dim(kspace, slab, 0, keepdims=False)[0]
    mask_one = lax.dynamic_index_in_dim(mask, slab, 0, keepdims=False)
    images = []
    for cascade in range(section_count):
        current = pair_block(
            current,
            sens_one,
            data_one,
            mask_one,
            all_steps[cascade],
            all_in[cascade],
            all_bias[cascade],
            all_out[cascade],
            half,
        )
        images.append(current)
    stacked = jnp.stack(images, axis=0)[:, None]
    arrived = lax.all_to_all(stacked, "section", split_axis=0, concat_axis=1, tiled=True)
    return arrived[:, ::2]


def solution(mesh):
    return jax.shard_map(
        body,
        mesh=mesh,
        in_specs=(
            P(None, "coil", "cuts", None, None),
            P(None, ("coil", "cuts"), None, None, None, None),
            P(None, ("coil", "cuts"), None, None, None, None),
            P(),
            P("section"),
            P("section", None, None),
            P("section", None),
            P("section", None, None),
        ),
        out_specs=P("section", None, "coil", "cuts", None, None),
        check_vma=False,
    )
```

profile of v0, /device:TPU:0, one launch (start us, length us, event | category | flops | bytes accessed | tf_op | source)
XLA Modules:
  0.0 516.5 jit_solution(3672511079097253560)
XLA Ops:
  7.8 2.3 all-gather
  12.5 32.9 %all-gather.14.cloned.1.call-done = bf16[1,32,80,2,128]{4,2,3,0,1:T(8,128)(2,1)} async-done(((bf16[1,8,80,2,128]{4,2,3,0,1:T(8,128)(2,1)}), bf16[1,32,80,2,128]{4,2,3,0,1:T(8,128)(2,1)}) %all-gather.14.cloned.1.call-update) | async-done | bytes 1310736 | tf_op jit(solution)/shard_map/all_gather | solution.py:161
  48.3 1.5 collective-permute-start
  51.0 1.6 constant_dynamic-slice_fusion
  52.6 4.5 collective-permute-done
  58.4 1.6 collective-permute-start.1
  60.5 5.9 %collective-permute-done.1 = bf16[16,40,2,128]{3,1,0,2:T(8,128)(2,1)S(1)} collective-permute-done((bf16[16,40,2,128]{3,1,0,2:T(8,128)(2,1)S(1)}, bf16[16,40,2,128]{3,1,0,2:T(8,128)(2,1)S(1)}, u32[]{:S(2)}, u32[]{:S(2)}) %collective-permute-start.1) | collective-permute-done | bytes 327712 | tf_op jit(solution)/shard_map/ppermute | solution.py:28
  75.5 7.9 %all-gather.2 = f32[4,1,128]{2,1,0:T(1,128)S(1)} all-gather(f32[1,1,128]{2,1,0:T(1,128)S(1)} %bitcast.665), channel_id=1, replica_groups=mesh['section'=4,'coil'=4,'cuts'=2] {'section'}, dimensions={0}, use_global_device_ids=true | all-gather | bytes 2560 | tf_op jit(solution)/shard_map/all_gather | solution.py:228
  83.4 8.1 %all_gather.39 = bf16[4,128,18]{1,2,0:T(8,128)(2,1)S(1)} all-gather(bf16[1,128,18]{1,2,0:T(8,128)(2,1)S(1)} %copy-done.37), channel_id=1, replica_groups=mesh['section'=4,'coil'=4,'cuts'=2] {'section'}, dimensions={0}, use_global_device_ids=true | all-gather | bytes 23040 | tf_op jit(solution)/shard_map/all_gather | solution.py:231
  91.5 8.9 %all-reduce.8 = f32[4]{0:T(128)S(1)} all-reduce(f32[4]{0:T(128)S(1)} %dynamic-update-slice), channel_id=1, replica_groups=mesh['section'=4,'coil'=4,'cuts'=2] {'section'}, use_global_device_ids=true, to_apply=%add.8 | all-reduce | flops 4 | bytes 32
  100.4 7.4 %all_gather.41 = bf16[4,18,128]{2,1,0:T(8,128)(2,1)S(1)} all-gather(bf16[1,18,128]{2,1,0:T(8,128)(2,1)S(1)} %copy-done.38), channel_id=1, replica_groups=mesh['section'=4,'coil'=4,'cuts'=2] {'section'}, dimensions={0}, use_global_device_ids=true | all-gather | bytes 23040 | tf_op jit(solution)/shard_map/all_gather | solution.py:232
  111.6 1.8 copy.168
  113.5 10.2 %convert_bitcast_fusion.3 = bf16[8,40,18,128]{3,2,1,0:T(8,128)(2,1)S(1)} fusion(f32[128]{0:T(128)S(1)} %get-tuple-element.73, bf16[8,40,18,128]{3,1,2,0:T(8,128)(2,1)} %bitcast.650, bf16[4,18,128]{2,1,0:T(8,128)(2,1)S(1)} %all_gather.41, bf16[4,128,18]{1,2,0:T(8,128)(2,1)S(1)} %all_gather.39), kind=kOutput, calls=%fused_computation.111 | convolution fusion | flops 409681920 | bytes 2961920 | tf_op jit(solution)/shard_map/fh,xyhz->xyfz/dot_general | solution.py:134
  125.1 1.7 collective-permute-start.6
  128.5 1.5 collective-permute-start.2
  130.5 5.0 collective-permute-done.2
  135.5 2.8 fusion.196
  138.2 2.0 all_gather.42
  141.1 32.4 %all-gather.8.cloned.1.call-done = bf16[32,80,2,128]{3,1,2,0:T(8,128)(2,1)} async-done(((bf16[8,80,2,128]{3,1,2,0:T(8,128)(2,1)}), bf16[32,80,2,128]{3,1,2,0:T(8,128)(2,1)}) %all-gather.8.cloned.1.call-update) | async-done | bytes 1310736 | tf_op jit(solution)/shard_map/all_gather | solution.py:161
  176.6 1.5 collective-permute-start.7
  178.1 7.3 %collective-permute-done.7 = bf16[16,40,2,128]{3,1,0,2:T(8,128)(2,1)S(1)} collective-permute-done((bf16[16,40,2,128]{3,1,0,2:T(8,128)(2,1)S(1)}, bf16[16,40,2,128]{3,1,0,2:T(8,128)(2,1)S(1)}, u32[]{:S(2)}, u32[]{:S(2)}) %collective-permute-start.7) | collective-permute-done | bytes 327712 | tf_op jit(solution)/shard_map/ppermute | solution.py:28
  186.8 1.5 collective-permute-start.8
  188.3 6.4 %collective-permute-done.8 = bf16[16,40,2,128]{3,1,0,2:T(8,128)(2,1)S(1)} collective-permute-done((bf16[16,40,2,128]{3,1,0,2:T(8,128)(2,1)S(1)}, bf16[16,40,2,128]{3,1,0,2:T(8,128)(2,1)S(1)}, u32[]{:S(2)}, u32[]{:S(2)}) %collective-permute-start.8) | collective-permute-done | bytes 327712 | tf_op jit(solution)/shard_map/ppermute | solution.py:28
  200.3 1.5 collective-permute-start.11
  201.8 1.6 collective-permute-done.11
  207.1 24.2 %reduce-scatter.13.cloned.1.call-done = bf16[8,80,2,128]{3,1,2,0:T(8,128)(2,1)} async-done(((bf16[32,80,2,128]{3,1,2,0:T(8,128)(2,1)}), bf16[8,80,2,128]{3,1,2,0:T(8,128)(2,1)}) %reduce-scatter.13.cloned.1.call-update) | async-done | bytes 327696 | tf_op jit(solution)/shard_map/reduce_scatter | solution.py:144
  231.2 1.8 copy.189
  233.1 10.2 %convert_bitcast_fusion.2 = bf16[8,40,18,128]{3,2,1,0:T(8,128)(2,1)S(1)} fusion(f32[128]{0:T(128)S(1)} %get-tuple-element.75, bf16[8,40,18,128]{3,1,2,0:T(8,128)(2,1)} %bitcast.651, bf16[4,18,128]{2,1,0:T(8,128)(2,1)} %copy-done.32, bf16[4,128,18]{1,2,0:T(8,128)(2,1)} %copy-done.31), kind=kOutput, calls=%fused_computation.110 | convolution fusion | flops 409681920 | bytes 2961920 | tf_op jit(solution)/shard_map/fh,xyhz->xyfz/dot_general | solution.py:134
  243.4 1.4 collective-permute-start.12
  244.8 1.7 collective-permute-start.13
  247.6 1.5 collective-permute-start.9
  249.5 5.0 collective-permute-done.9
  254.5 2.7 fusion.197
  257.3 2.0 all_gather.44
  260.2 31.6 %all-gather.10.cloned.1.call-done = bf16[32,80,2,128]{3,1,2,0:T(8,128)(2,1)} async-done(((bf16[8,80,2,128]{3,1,2,0:T(8,128)(2,1)}), bf16[32,80,2,128]{3,1,2,0:T(8,128)(2,1)}) %all-gather.10.cloned.1.call-update) | async-done | bytes 1310736 | tf_op jit(solution)/shard_map/all_gather | solution.py:161
  294.9 1.5 collective-permute-start.14
  296.4 7.3 %collective-permute-done.14 = bf16[16,40,2,128]{3,1,0,2:T(8,128)(2,1)S(1)} collective-permute-done((bf16[16,40,2,128]{3,1,0,2:T(8,128)(2,1)S(1)}, bf16[16,40,2,128]{3,1,0,2:T(8,128)(2,1)S(1)}, u32[]{:S(2)}, u32[]{:S(2)}) %collective-permute-start.14) | collective-permute-done | bytes 327712 | tf_op jit(solution)/shard_map/ppermute | solution.py:28
  305.1 1.5 collective-permute-start.15
  306.6 6.4 %collective-permute-done.15 = bf16[16,40,2,128]{3,1,0,2:T(8,128)(2,1)S(1)} collective-permute-done((bf16[16,40,2,128]{3,1,0,2:T(8,128)(2,1)S(1)}, bf16[16,40,2,128]{3,1,0,2:T(8,128)(2,1)S(1)}, u32[]{:S(2)}, u32[]{:S(2)}) %collective-permute-start.15) | collective-permute-done | bytes 327712 | tf_op jit(solution)/shard_map/ppermute | solution.py:28
  319.9 1.8 collective-permute-done.18
  325.4 24.1 %reduce-scatter.17.cloned.1.call-done = bf16[8,80,2,128]{3,1,2,0:T(8,128)(2,1)} async-done(((bf16[32,80,2,128]{3,1,2,0:T(8,128)(2,1)}), bf16[8,80,2,128]{3,1,2,0:T(8,128)(2,1)}) %reduce-scatter.17.cloned.1.call-update) | async-done | bytes 327696 | tf_op jit(solution)/shard_map/reduce_scatter | solution.py:144
  349.5 1.8 copy.209
  351.6 10.2 %convert_bitcast_fusion.1 = bf16[8,40,18,128]{3,2,1,0:T(8,128)(2,1)S(1)} fusion(f32[128]{0:T(128)S(1)} %get-tuple-element.74, bf16[8,40,18,128]{3,1,2,0:T(8,128)(2,1)} %bitcast.652, bf16[4,18,128]{2,1,0:T(8,128)(2,1)} %copy-done.32, bf16[4,128,18]{1,2,0:T(8,128)(2,1)} %copy-done.31), kind=kOutput, calls=%fused_computation.109 | convolution fusion | flops 409681920 | bytes 2961920 | tf_op jit(solution)/shard_map/fh,xyhz->xyfz/dot_general | solution.py:134
  361.9 1.4 collective-permute-start.19
  365.6 1.5 collective-permute-start.16
  367.6 5.0 collective-permute-done.16
  372.6 2.7 fusion.198
  375.3 2.0 all_gather.46
  378.2 31.6 %all-gather.12.cloned.1.call-done = bf16[32,80,2,128]{3,1,2,0:T(8,128)(2,1)} async-done(((bf16[8,80,2,128]{3,1,2,0:T(8,128)(2,1)}), bf16[32,80,2,128]{3,1,2,0:T(8,128)(2,1)}) %all-gather.12.cloned.1.call-update) | async-done | bytes 1310736 | tf_op jit(solution)/shard_map/all_gather | solution.py:161
  412.9 1.5 collective-permute-start.21
  414.4 7.3 %collective-permute-done.21 = bf16[16,40,2,128]{3,1,0,2:T(8,128)(2,1)S(1)} collective-permute-done((bf16[16,40,2,128]{3,1,0,2:T(8,128)(2,1)S(1)}, bf16[16,40,2,128]{3,1,0,2:T(8,128)(2,1)S(1)}, u32[]{:S(2)}, u32[]{:S(2)}) %collective-permute-start.21) | collective-permute-done | bytes 327712 | tf_op jit(solution)/shard_map/ppermute | solution.py:28
  423.1 1.5 collective-permute-start.22
  424.6 6.4 %collective-permute-done.22 = bf16[16,40,2,128]{3,1,0,2:T(8,128)(2,1)S(1)} collective-permute-done((bf16[16,40,2,128]{3,1,0,2:T(8,128)(2,1)S(1)}, bf16[16,40,2,128]{3,1,0,2:T(8,128)(2,1)S(1)}, u32[]{:S(2)}, u32[]{:S(2)}) %collective-permute-start.22) | collective-permute-done | bytes 327712 | tf_op jit(solution)/shard_map/ppermute | solution.py:28
  436.6 1.5 collective-permute-start.25
  438.1 1.5 collective-permute-done.25
  443.4 24.2 %reduce-scatter.21.cloned.1.call-done = bf16[8,80,2,128]{3,1,2,0:T(8,128)(2,1)} async-done(((bf16[32,80,2,128]{3,1,2,0:T(8,128)(2,1)}), bf16[8,80,2,128]{3,1,2,0:T(8,128)(2,1)}) %reduce-scatter.21.cloned.1.call-update) | async-done | bytes 327696 | tf_op jit(solution)/shard_map/reduce_scatter | solution.py:144
  467.5 1.8 copy.229
  469.4 10.2 %convert_bitcast_fusion = bf16[8,40,18,128]{3,2,1,0:T(8,128)(2,1)S(1)} fusion(f32[128]{0:T(128)S(1)} %get-tuple-element.76, bf16[8,40,18,128]{3,1,2,0:T(8,128)(2,1)} %bitcast.649, bf16[4,18,128]{2,1,0:T(8,128)(2,1)} %copy-done.32, bf16[4,128,18]{1,2,0:T(8,128)(2,1)} %copy-done.31), kind=kOutput, calls=%fused_computation.108 | convolution fusion | flops 409681920 | bytes 2961920 | tf_op jit(solution)/shard_map/fh,xyhz->xyfz/dot_general | solution.py:134
  479.6 1.3 collective-permute-start.26
  481.0 1.5 collective-permute-start.27
  483.6 1.5 collective-permute-start.23
  485.6 5.0 collective-permute-done.23
  490.6 2.7 fusion.240
  494.6 13.7 %all_to_all.12 = bf16[4,1,8,40,2,128]{5,4,3,2,1,0:T(2,128)(2,1)S(1)} all-to-all(bf16[4,1,8,40,2,128]{5,4,3,2,1,0:T(2,128)(2,1)S(1)} %maximum_bitcast_fusion), channel_id=1, replica_groups=mesh['section'=4,'coil'=4,'cuts'=2] {'section'}, dimensions={0} | all-to-all | bytes 1310720 | tf_op jit(solution)/shard_map/all_to_all | solution.py:255
  (316 shorter events, 77.2 us)
Async XLA Ops:
  6.5 38.8 %all-gather.14.cloned.1.call-start = ((), (), s32[]{:S(2)}) async-start(), calls=%async_computation.20 | async-start | bytes 1638400 | tf_op jit(solution)/shard_map/all_gather | solution.py:161
  10.1 101.5 %reduce-scatter.9.cloned.1.call-start = ((), (), s32[]{:S(2)}) async-start(), calls=%async_computation.9 | async-start | bytes 1638400 | tf_op jit(solution)/shard_map/reduce_scatter | solution.py:144
  12.2 35.2 %copy-start.11 = (bf16[128,128]{1,0:T(8,128)(2,1)}, bf16[128,128]{1,0:T(8,128)(2,1)S(1)}, u32[]{:S(2)}) copy-start(bf16[128,128]{1,0:T(8,128)(2,1)S(1)} %multiply_convert_fusion.2) | copy-start | bytes 98308
  12.5 34.9 %copy-start.15 = (bf16[128,128]{1,0:T(8,128)(2,1)}, bf16[128,128]{1,0:T(8,128)(2,1)S(1)}, u32[]{:S(2)}) copy-start(bf16[128,128]{1,0:T(8,128)(2,1)S(1)} %get-tuple-element.89) | copy-start | bytes 98308
  48.3 8.8 %collective-permute-start = (bf16[16,40,2,128]{3,1,0,2:T(8,128)(2,1)S(1)}, bf16[16,40,2,128]{3,1,0,2:T(8,128)(2,1)S(1)}, u32[]{:S(2)}, u32[]{:S(2)}) collective-permute-start(bf16[16,40,2,128]{3,1,0,2:T(8,128)(2,1)S(1)} %dynamic-slice_bitcast_fusion.8), channel_id=1, source_target_pairs={{0,8},{8,0},{16,24},{24,16},{1,9},{9,1},{17,25},{25,17},{2,10},{10... | collective-permute-start | bytes 983048 | tf_op jit(solution)/shard_map/ppermute | solution.py:28
  50.1 7.2 %copy-start.19 = (bf16[2,32,2,32,1]{1,3,0,4,2:T(8,128)(2,1)}, bf16[2,32,2,32,1]{1,3,0,4,2:T(8,128)(2,1)S(1)}, u32[]{:S(2)}) copy-start(bf16[2,32,2,32,1]{1,3,0,4,2:T(8,128)(2,1)S(1)} %copy.238) | copy-start | bytes 24580
  51.0 6.3 %copy-start.33 = (f32[40,128]{1,0:T(8,128)}, f32[40,128]{1,0:T(8,128)S(1)}, u32[]{:S(2)}) copy-start(f32[40,128]{1,0:T(8,128)S(1)} %convert_bitcast_fusion.4) | copy-start | bytes 61444
  58.4 8.0 %collective-permute-start.1 = (bf16[16,40,2,128]{3,1,0,2:T(8,128)(2,1)S(1)}, bf16[16,40,2,128]{3,1,0,2:T(8,128)(2,1)S(1)}, u32[]{:S(2)}, u32[]{:S(2)}) collective-permute-start(bf16[16,40,2,128]{3,1,0,2:T(8,128)(2,1)S(1)} %dynamic-slice_bitcast_fusion.7), channel_id=1, source_target_pairs={{0,8},{8,0},{16,24},{24,16},{1,9},{9,1},{17,25},{25,17},{2,10},{10... | collective-permute-start | bytes 983048 | tf_op jit(solution)/shard_map/ppermute | solution.py:28
  60.5 7.0 %copy-start.23 = (bf16[128,128]{1,0:T(8,128)(2,1)}, bf16[128,128]{1,0:T(8,128)(2,1)S(1)}, u32[]{:S(2)}) copy-start(bf16[128,128]{1,0:T(8,128)(2,1)S(1)} %get-tuple-element.91) | copy-start | bytes 98308
  60.5 7.0 %copy-start.27 = (bf16[128,128]{1,0:T(8,128)(2,1)}, bf16[128,128]{1,0:T(8,128)(2,1)S(1)}, u32[]{:S(2)}) copy-start(bf16[128,128]{1,0:T(8,128)(2,1)S(1)} %get-tuple-element.92) | copy-start | bytes 98308
  70.6 12.7 %copy-start.37 = (bf16[1,128,18]{1,2,0:T(8,128)(2,1)S(1)}, bf16[1,128,18]{1,2,0:T(8,128)(2,1)}, u32[]{:S(2)}) copy-start(bf16[1,128,18]{1,2,0:T(8,128)(2,1)} %param.13) | copy-start | bytes 13828
  70.6 29.8 %copy-start.38 = (bf16[1,18,128]{2,1,0:T(8,128)(2,1)S(1)}, bf16[1,18,128]{2,1,0:T(8,128)(2,1)}, u32[]{:S(2)}) copy-start(bf16[1,18,128]{2,1,0:T(8,128)(2,1)} %param.15) | copy-start | bytes 13828
  70.7 56.7 %reduce-scatter.11.cloned.1.call-start = ((), (), s32[]{:S(2)}) async-start(), calls=%async_computation.10 | async-start | bytes 491520 | tf_op jit(solution)/shard_map/reduce_scatter | solution.py:150
  70.9 37.0 %collective-permute-start.3 = (bf16[8,1,2,128]{3,2,1,0:T(2,128)(2,1)S(1)}, bf16[8,1,2,128]{3,2,1,0:T(2,128)(2,1)S(1)}, u32[]{:S(2)}, u32[]{:S(2)}) collective-permute-start(bf16[8,1,2,128]{3,2,1,0:T(2,128)(2,1)S(1)} %get-tuple-element.67), channel_id=1, source_target_pairs={{0,1},{2,3},{4,5},{6,7},{8,9},{10,11},{12,13},{14,15},{16,17},{18,... | collective-permute-start | bytes 12296 | tf_op jit(solution)/shard_map/ppermute | solution.py:15
  72.2 35.7 %collective-permute-start.4 = (bf16[8,1,2,128]{3,2,1,0:T(2,128)(2,1)S(1)}, bf16[8,1,2,128]{3,2,1,0:T(2,128)(2,1)S(1)}, u32[]{:S(2)}, u32[]{:S(2)}) collective-permute-start(bf16[8,1,2,128]{3,2,1,0:T(2,128)(2,1)S(1)} %get-tuple-element.68), channel_id=1, source_target_pairs={{1,0},{3,2},{5,4},{7,6},{9,8},{11,10},{13,12},{15,14},{17,16},{19,... | collective-permute-start | bytes 12296 | tf_op jit(solution)/shard_map/ppermute | solution.py:16
  91.5 22.0 %copy-start.31 = (bf16[4,128,18]{1,2,0:T(8,128)(2,1)}, bf16[4,128,18]{1,2,0:T(8,128)(2,1)S(1)}, u32[]{:S(2)}) copy-start(bf16[4,128,18]{1,2,0:T(8,128)(2,1)S(1)} %all_gather.39) | copy-start | bytes 55300
  107.9 5.6 %copy-start.32 = (bf16[4,18,128]{2,1,0:T(8,128)(2,1)}, bf16[4,18,128]{2,1,0:T(8,128)(2,1)S(1)}, u32[]{:S(2)}) copy-start(bf16[4,18,128]{2,1,0:T(8,128)(2,1)S(1)} %all_gather.41) | copy-start | bytes 55300
  113.4 60.1 %all-gather.8.cloned.1.call-start = ((), (), s32[]{:S(2)}) async-start(), calls=%async_computation.11 | async-start | bytes 1638400 | tf_op jit(solution)/shard_map/all_gather | solution.py:161
  123.8 6.2 %collective-permute-start.5 = (bf16[8,1,18,128]{3,2,1,0:T(8,128)(2,1)S(1)}, bf16[8,1,18,128]{3,2,1,0:T(8,128)(2,1)S(1)}, u32[]{:S(2)}, u32[]{:S(2)}) collective-permute-start(bf16[8,1,18,128]{3,2,1,0:T(8,128)(2,1)S(1)} %get-tuple-element.25), channel_id=1, source_target_pairs={{0,1},{2,3},{4,5},{6,7},{8,9},{10,11},{12,13},{14,15},{16,17},{18,... | collective-permute-start | bytes 110600 | tf_op jit(solution)/shard_map/ppermute | solution.py:15
  125.1 4.9 collective-permute-start.6
  128.5 7.0 %copy-start.3 = (bf16[8,40,2,128]{3,0,2,1:T(8,128)(2,1)S(1)}, bf16[8,40,2,128]{3,0,2,1:T(8,128)(2,1)}, u32[]{:S(2)}) copy-start(bf16[8,40,2,128]{3,0,2,1:T(8,128)(2,1)} %reduce-scatter.11.cloned.1.call-done) | copy-start | bytes 491524
  128.5 7.0 %collective-permute-start.2 = (bf16[8,40,2,128]{3,2,1,0:T(2,128)(2,1)S(1)}, bf16[8,40,2,128]{3,2,1,0:T(2,128)(2,1)S(1)}, u32[]{:S(2)}, u32[]{:S(2)}) collective-permute-start(bf16[8,40,2,128]{3,2,1,0:T(2,128)(2,1)S(1)} %copy.169), channel_id=1, source_target_pairs={{0,8},{8,0},{16,24},{24,16},{1,9},{9,1},{17,25},{25,17},{2,10},{10... | collective-permute-start | bytes 491528 | tf_op jit(solution)/shard_map/ppermute | solution.py:28
  141.1 90.2 %reduce-scatter.13.cloned.1.call-start = ((), (), s32[]{:S(2)}) async-start(), calls=%async_computation.12 | async-start | bytes 1638400 | tf_op jit(solution)/shard_map/reduce_scatter | solution.py:144
  176.6 9.0 %copy-start.8 = (bf16[1,1,32,40,2,128]{5,4,3,2,1,0:T(2,128)(2,1)S(1)}, bf16[1,1,32,40,2,128]{5,4,3,2,1,0:T(2,128)(2,1)}, u32[]{:S(2)}) copy-start(bf16[1,1,32,40,2,128]{5,4,3,2,1,0:T(2,128)(2,1)} %copy-done.7) | copy-start | bytes 1966084
  176.6 9.0 %copy-start.20 = (bf16[2,32,2,32,1]{1,3,0,4,2:T(8,128)(2,1)S(1)}, bf16[2,32,2,32,1]{1,3,0,4,2:T(8,128)(2,1)}, u32[]{:S(2)}) copy-start(bf16[2,32,2,32,1]{1,3,0,4,2:T(8,128)(2,1)} %copy-done.19) | copy-start | bytes 24580
  176.6 9.0 %copy-start.34 = (f32[40,128]{1,0:T(8,128)S(1)}, f32[40,128]{1,0:T(8,128)}, u32[]{:S(2)}) copy-start(f32[40,128]{1,0:T(8,128)} %copy-done.33) | copy-start | bytes 61444
  176.6 8.8 %collective-permute-start.7 = (bf16[16,40,2,128]{3,1,0,2:T(8,128)(2,1)S(1)}, bf16[16,40,2,128]{3,1,0,2:T(8,128)(2,1)S(1)}, u32[]{:S(2)}, u32[]{:S(2)}) collective-permute-start(bf16[16,40,2,128]{3,1,0,2:T(8,128)(2,1)S(1)} %dynamic-slice_bitcast_fusion.6), channel_id=1, source_target_pairs={{0,8},{8,0},{16,24},{24,16},{1,9},{9,1},{17,25},{25,17},{2,10},{10... | collective-permute-start | bytes 983048 | tf_op jit(solution)/shard_map/ppermute | solution.py:28
  186.8 7.9 %collective-permute-start.8 = (bf16[16,40,2,128]{3,1,0,2:T(8,128)(2,1)S(1)}, bf16[16,40,2,128]{3,1,0,2:T(8,128)(2,1)S(1)}, u32[]{:S(2)}, u32[]{:S(2)}) collective-permute-start(bf16[16,40,2,128]{3,1,0,2:T(8,128)(2,1)S(1)} %dynamic-slice_bitcast_fusion.5), channel_id=1, source_target_pairs={{0,8},{8,0},{16,24},{24,16},{1,9},{9,1},{17,25},{25,17},{2,10},{10... | collective-permute-start | bytes 983048 | tf_op jit(solution)/shard_map/ppermute | solution.py:28
  199.0 47.5 %reduce-scatter.15.cloned.1.call-start = ((), (), s32[]{:S(2)}) async-start(), calls=%async_computation.13 | async-start | bytes 491520 | tf_op jit(solution)/shard_map/reduce_scatter | solution.py:150
  199.0 2.8 collective-permute-start.10
  200.3 3.1 collective-permute-start.11
  233.1 58.7 %all-gather.10.cloned.1.call-start = ((), (), s32[]{:S(2)}) async-start(), calls=%async_computation.14 | async-start | bytes 1638400 | tf_op jit(solution)/shard_map/all_gather | solution.py:161
  243.4 5.7 %collective-permute-start.12 = (bf16[8,1,18,128]{3,2,1,0:T(8,128)(2,1)S(1)}, bf16[8,1,18,128]{3,2,1,0:T(8,128)(2,1)S(1)}, u32[]{:S(2)}, u32[]{:S(2)}) collective-permute-start(bf16[8,1,18,128]{3,2,1,0:T(8,128)(2,1)S(1)} %get-tuple-element.21), channel_id=1, source_target_pairs={{0,1},{2,3},{4,5},{6,7},{8,9},{10,11},{12,13},{14,15},{16,17},{18,... | collective-permute-start | bytes 110600 | tf_op jit(solution)/shard_map/ppermute | solution.py:15
  244.8 4.3 collective-permute-start.13
  247.6 7.0 %copy-start.5 = (bf16[8,40,2,128]{3,0,2,1:T(8,128)(2,1)S(1)}, bf16[8,40,2,128]{3,0,2,1:T(8,128)(2,1)}, u32[]{:S(2)}) copy-start(bf16[8,40,2,128]{3,0,2,1:T(8,128)(2,1)} %reduce-scatter.15.cloned.1.call-done) | copy-start | bytes 491524
  247.6 7.0 %collective-permute-start.9 = (bf16[8,40,2,128]{3,2,1,0:T(2,128)(2,1)S(1)}, bf16[8,40,2,128]{3,2,1,0:T(2,128)(2,1)S(1)}, u32[]{:S(2)}, u32[]{:S(2)}) collective-permute-start(bf16[8,40,2,128]{3,2,1,0:T(2,128)(2,1)S(1)} %copy.190), channel_id=1, source_target_pairs={{0,8},{8,0},{16,24},{24,16},{1,9},{9,1},{17,25},{25,17},{2,10},{10... | collective-permute-start | bytes 491528 | tf_op jit(solution)/shard_map/ppermute | solution.py:28
  260.1 89.4 %reduce-scatter.17.cloned.1.call-start = ((), (), s32[]{:S(2)}) async-start(), calls=%async_computation.15 | async-start | bytes 1638400 | tf_op jit(solution)/shard_map/reduce_scatter | solution.py:144
  294.8 9.1 %copy-start.9 = (bf16[1,1,32,40,2,128]{5,4,3,2,1,0:T(2,128)(2,1)S(1)}, bf16[1,1,32,40,2,128]{5,4,3,2,1,0:T(2,128)(2,1)}, u32[]{:S(2)}) copy-start(bf16[1,1,32,40,2,128]{5,4,3,2,1,0:T(2,128)(2,1)} %copy-done.7) | copy-start | bytes 1966084
  294.8 9.1 %copy-start.21 = (bf16[2,32,2,32,1]{1,3,0,4,2:T(8,128)(2,1)S(1)}, bf16[2,32,2,32,1]{1,3,0,4,2:T(8,128)(2,1)}, u32[]{:S(2)}) copy-start(bf16[2,32,2,32,1]{1,3,0,4,2:T(8,128)(2,1)} %copy-done.19) | copy-start | bytes 24580
  294.9 9.1 %copy-start.35 = (f32[40,128]{1,0:T(8,128)S(1)}, f32[40,128]{1,0:T(8,128)}, u32[]{:S(2)}) copy-start(f32[40,128]{1,0:T(8,128)} %copy-done.33) | copy-start | bytes 61444
  294.9 8.8 %collective-permute-start.14 = (bf16[16,40,2,128]{3,1,0,2:T(8,128)(2,1)S(1)}, bf16[16,40,2,128]{3,1,0,2:T(8,128)(2,1)S(1)}, u32[]{:S(2)}, u32[]{:S(2)}) collective-permute-start(bf16[16,40,2,128]{3,1,0,2:T(8,128)(2,1)S(1)} %dynamic-slice_bitcast_fusion.4), channel_id=1, source_target_pairs={{0,8},{8,0},{16,24},{24,16},{1,9},{9,1},{17,25},{25,17},{2,10},{10... | collective-permute-start | bytes 983048 | tf_op jit(solution)/shard_map/ppermute | solution.py:28
  305.1 8.0 %collective-permute-start.15 = (bf16[16,40,2,128]{3,1,0,2:T(8,128)(2,1)S(1)}, bf16[16,40,2,128]{3,1,0,2:T(8,128)(2,1)S(1)}, u32[]{:S(2)}, u32[]{:S(2)}) collective-permute-start(bf16[16,40,2,128]{3,1,0,2:T(8,128)(2,1)S(1)} %dynamic-slice_bitcast_fusion.3), channel_id=1, source_target_pairs={{0,8},{8,0},{16,24},{24,16},{1,9},{9,1},{17,25},{25,17},{2,10},{10... | collective-permute-start | bytes 983048 | tf_op jit(solution)/shard_map/ppermute | solution.py:28
  317.3 47.3 %reduce-scatter.19.cloned.1.call-start = ((), (), s32[]{:S(2)}) async-start(), calls=%async_computation.16 | async-start | bytes 491520 | tf_op jit(solution)/shard_map/reduce_scatter | solution.py:150
  317.3 2.6 collective-permute-start.17
  318.6 3.1 collective-permute-start.18
  351.4 58.5 %all-gather.12.cloned.1.call-start = ((), (), s32[]{:S(2)}) async-start(), calls=%async_computation.17 | async-start | bytes 1638400 | tf_op jit(solution)/shard_map/all_gather | solution.py:161
  361.9 5.3 %collective-permute-start.19 = (bf16[8,1,18,128]{3,2,1,0:T(8,128)(2,1)S(1)}, bf16[8,1,18,128]{3,2,1,0:T(8,128)(2,1)S(1)}, u32[]{:S(2)}, u32[]{:S(2)}) collective-permute-start(bf16[8,1,18,128]{3,2,1,0:T(8,128)(2,1)S(1)} %get-tuple-element.15), channel_id=1, source_target_pairs={{0,1},{2,3},{4,5},{6,7},{8,9},{10,11},{12,13},{14,15},{16,17},{18,... | collective-permute-start | bytes 110600 | tf_op jit(solution)/shard_map/ppermute | solution.py:15
  363.2 3.9 collective-permute-start.20
  365.6 7.0 %copy-start.6 = (bf16[8,40,2,128]{3,0,2,1:T(8,128)(2,1)S(1)}, bf16[8,40,2,128]{3,0,2,1:T(8,128)(2,1)}, u32[]{:S(2)}) copy-start(bf16[8,40,2,128]{3,0,2,1:T(8,128)(2,1)} %reduce-scatter.19.cloned.1.call-done) | copy-start | bytes 491524
  365.6 7.0 %collective-permute-start.16 = (bf16[8,40,2,128]{3,2,1,0:T(2,128)(2,1)S(1)}, bf16[8,40,2,128]{3,2,1,0:T(2,128)(2,1)S(1)}, u32[]{:S(2)}, u32[]{:S(2)}) collective-permute-start(bf16[8,40,2,128]{3,2,1,0:T(2,128)(2,1)S(1)} %copy.210), channel_id=1, source_target_pairs={{0,8},{8,0},{16,24},{24,16},{1,9},{9,1},{17,25},{25,17},{2,10},{10... | collective-permute-start | bytes 491528 | tf_op jit(solution)/shard_map/ppermute | solution.py:28
  378.1 89.4 %reduce-scatter.21.cloned.1.call-start = ((), (), s32[]{:S(2)}) async-start(), calls=%async_computation.18 | async-start | bytes 1638400 | tf_op jit(solution)/shard_map/reduce_scatter | solution.py:144
  412.9 9.0 %copy-start.10 = (bf16[1,1,32,40,2,128]{5,4,3,2,1,0:T(2,128)(2,1)S(1)}, bf16[1,1,32,40,2,128]{5,4,3,2,1,0:T(2,128)(2,1)}, u32[]{:S(2)}) copy-start(bf16[1,1,32,40,2,128]{5,4,3,2,1,0:T(2,128)(2,1)} %copy-done.7) | copy-start | bytes 1966084
  412.9 9.0 %copy-start.22 = (bf16[2,32,2,32,1]{1,3,0,4,2:T(8,128)(2,1)S(1)}, bf16[2,32,2,32,1]{1,3,0,4,2:T(8,128)(2,1)}, u32[]{:S(2)}) copy-start(bf16[2,32,2,32,1]{1,3,0,4,2:T(8,128)(2,1)} %copy-done.19) | copy-start | bytes 24580
  412.9 9.0 %copy-start.36 = (f32[40,128]{1,0:T(8,128)S(1)}, f32[40,128]{1,0:T(8,128)}, u32[]{:S(2)}) copy-start(f32[40,128]{1,0:T(8,128)} %copy-done.33) | copy-start | bytes 61444
  412.9 8.8 %collective-permute-start.21 = (bf16[16,40,2,128]{3,1,0,2:T(8,128)(2,1)S(1)}, bf16[16,40,2,128]{3,1,0,2:T(8,128)(2,1)S(1)}, u32[]{:S(2)}, u32[]{:S(2)}) collective-permute-start(bf16[16,40,2,128]{3,1,0,2:T(8,128)(2,1)S(1)} %dynamic-slice_bitcast_fusion.2), channel_id=1, source_target_pairs={{0,8},{8,0},{16,24},{24,16},{1,9},{9,1},{17,25},{25,17},{2,10},{10... | collective-permute-start | bytes 983048 | tf_op jit(solution)/shard_map/ppermute | solution.py:28
  423.1 7.9 %collective-permute-start.22 = (bf16[16,40,2,128]{3,1,0,2:T(8,128)(2,1)S(1)}, bf16[16,40,2,128]{3,1,0,2:T(8,128)(2,1)S(1)}, u32[]{:S(2)}, u32[]{:S(2)}) collective-permute-start(bf16[16,40,2,128]{3,1,0,2:T(8,128)(2,1)S(1)} %dynamic-slice_bitcast_fusion.1), channel_id=1, source_target_pairs={{0,8},{8,0},{16,24},{24,16},{1,9},{9,1},{17,25},{25,17},{2,10},{10... | collective-permute-start | bytes 983048 | tf_op jit(solution)/shard_map/ppermute | solution.py:28
  435.3 47.3 %reduce-scatter.23.cloned.1.call-start = ((), (), s32[]{:S(2)}) async-start(), calls=%async_computation.19 | async-start | bytes 491520 | tf_op jit(solution)/shard_map/reduce_scatter | solution.py:150
  435.3 2.8 collective-permute-start.24
  436.6 3.1 collective-permute-start.25
  479.6 5.5 %collective-permute-start.26 = (bf16[8,1,18,128]{3,2,1,0:T(8,128)(2,1)S(1)}, bf16[8,1,18,128]{3,2,1,0:T(8,128)(2,1)S(1)}, u32[]{:S(2)}, u32[]{:S(2)}) collective-permute-start(bf16[8,1,18,128]{3,2,1,0:T(8,128)(2,1)S(1)} %get-tuple-element.9), channel_id=1, source_target_pairs={{0,1},{2,3},{4,5},{6,7},{8,9},{10,11},{12,13},{14,15},{16,17},{18,... | collective-permute-start | bytes 110600 | tf_op jit(solution)/shard_map/ppermute | solution.py:15
  481.0 4.2 collective-permute-start.27
  483.6 7.0 %copy-start.4 = (bf16[8,40,2,128]{3,0,2,1:T(8,128)(2,1)S(1)}, bf16[8,40,2,128]{3,0,2,1:T(8,128)(2,1)}, u32[]{:S(2)}) copy-start(bf16[8,40,2,128]{3,0,2,1:T(8,128)(2,1)} %reduce-scatter.23.cloned.1.call-done) | copy-start | bytes 491524
  483.6 7.0 %collective-permute-start.23 = (bf16[8,40,2,128]{3,2,1,0:T(2,128)(2,1)S(1)}, bf16[8,40,2,128]{3,2,1,0:T(2,128)(2,1)S(1)}, u32[]{:S(2)}, u32[]{:S(2)}) collective-permute-start(bf16[8,40,2,128]{3,2,1,0:T(2,128)(2,1)S(1)} %copy.230), channel_id=1, source_target_pairs={{0,8},{8,0},{16,24},{24,16},{1,9},{9,1},{17,25},{25,17},{2,10},{10... | collective-permute-start | bytes 491528 | tf_op jit(solution)/shard_map/ppermute | solution.py:28
  493.3 15.8 %copy-start.1 = (bf16[2,1,32,80,2,128]{5,4,3,2,1,0:T(2,128)(2,1)S(1)}, bf16[2,1,32,80,2,128]{5,4,3,2,1,0:T(2,128)(2,1)}, u32[]{:S(2)}) copy-start(bf16[2,1,32,80,2,128]{5,4,3,2,1,0:T(2,128)(2,1)} %param.9) | copy-start | bytes 7864324
  (17 other events, 30.4 us)
Sparse Core Ops, SparseCore 0:
  10.2 35.1 all-gather.13
  70.8 32.0 reduce-scatter.8
  113.6 7.5 reduce-scatter.10
  141.2 32.3 all-gather.7
  199.1 32.1 reduce-scatter.12
  233.3 6.4 reduce-scatter.14
  260.2 31.5 all-gather.9
  317.4 32.0 reduce-scatter.16
  351.8 6.4 reduce-scatter.18
  378.3 31.5 all-gather.11
  435.4 32.1 reduce-scatter.20
  469.6 6.4 reduce-scatter.22
where the time goes:
time: 525 us; the launch traced here: 516 us
  waiting for transfers between devices  278 us (53%)
  blocking collectives  54.4 us (10%)
  matrix products  49.7 us (9%)
  local copies, waits for them, and re-layouts  44.4 us (8%)
  starting transfers between devices  41.4 us (8%)
  other arithmetic  32.6 us (6%)
  between operations  16.4 us (3%)
    all_gather x4, waiting for transfers between devices, pair_block(): whole = lax.all_gather(halves, 'coil', axis=0, tiled=True)  129 us
    reduce_scatter x4, waiting for transfers between devices, sum_gradient(): lax.psum_scatter(back_rows(jnp.int32(0), lax.axis_size('coil') * current....  72.5 us
    ppermute x12, waiting for transfers between devices, from_partner(): return lax.ppermute(block, axis, route)  71.4 us
    dot_general x4, matrix products, refine_rows(): jnp.einsum('fh,xyhz->xyfz', weights_out, hidden, preferred_element_type=j...  40.9 us
    ppermute x12, starting transfers between devices, from_partner(): return lax.ppermute(block, axis, route)  18.4 us
    all_to_all x1, blocking collectives, body(): lax.all_to_all(stacked, 'section', split_axis=0, concat_axis=1, tiled=True)  13.7 us
    ppermute x8, starting transfers between devices, extended_2(): after = lax.ppermute(leading, axis, down)  11.8 us
    ppermute x8, starting transfers between devices, extended_2(): before = lax.ppermute(last, axis, up)  10.5 us
  transfers between devices with their start and end apart: 40, of which 22 were waited for; matrix products, arithmetic and copies ran while one was open for 13% of the time, Pallas kernels for 0%

commit v1 on v0

--- a/solution.py
+++ b/solution.py
@@ -158,7 +158,12 @@
 
 def pair_block(current, sens_one, data_one, mask_one, step, weights_in, bias, weights_out, half):
     halves = whole_rows(current)
-    whole = lax.all_gather(halves, "coil", axis=0, tiled=True)
+    ring = [halves]
+    for hop in range(3):
+        ring.append(lax.ppermute(ring[-1], "coil", [(dev, (dev + 1) % 4) for dev in range(4)]))
+    whole = jnp.roll(
+        jnp.concatenate(ring[::-1], axis=0), (lax.axis_index("coil") + 1) * ring[0].shape[0], axis=0
+    )
     size_x, size_y, _, size_z = whole.shape
     half_x = size_x // 2
     half_y = size_y // 2

time: 525 us -> 510 us (0.971)
  waiting for transfers between devices: 278 us -> 258 us
  other arithmetic: 32.6 us -> 25.7 us
    all_gather x4 -> x0, waiting for transfers between devices: 129 us -> none  [pair_block(): whole = lax.all_gather(halves, 'coil', axis=0, tiled=True)]
    ppermute x0 -> x12, waiting for transfers between devices: none -> 126 us  [pair_block(): lax.ppermute(ring[-1], 'coil', [(dev, (dev + 1) % 4) for dev in range(4)])]
    ppermute x12, waiting for transfers between devices: 71.4 us -> 59.9 us  [from_partner(): return lax.ppermute(block, axis, route)]
    dot_general x0 -> x4, local copies, waits for them, and re-layouts: none -> 6.95 us  [refine_rows(): jnp.einsum('fh,xyhz->xyfz', weights_out, hidden, preferred_element_type=j...]
    reduce_scatter x4, waiting for transfers between devices: 72.5 us -> 66.9 us  [sum_gradient(): lax.psum_scatter(back_rows(jnp.int32(0), lax.axis_size('coil') * current....]
  transfers between devices with their start and end apart: 40 -> 48, of which waited for: 22 -> 30; matrix products, arithmetic and copies ran while one was open for 13% -> 16% of each run, Pallas kernels for 0% -> 0%
where the time goes in v1:
time: 510 us; the launch traced here: 500 us
  waiting for transfers between devices  258 us (51%)
  blocking collectives  54.8 us (11%)
  matrix products  53.9 us (11%)
  local copies, waits for them, and re-layouts  46.6 us (9%)
  starting transfers between devices  45 us (9%)
  other arithmetic  25.7 us (5%)
  between operations  16.3 us (3%)
    ppermute x12, waiting for transfers between devices, pair_block(): lax.ppermute(ring[-1], 'coil', [(dev, (dev + 1) % 4) for dev in range(4)])  126 us
    reduce_scatter x4, waiting for transfers between devices, sum_gradient(): lax.psum_scatter(back_rows(jnp.int32(0), lax.axis_size('coil') * current....  66.9 us
    ppermute x12, waiting for transfers between devices, from_partner(): return lax.ppermute(block, axis, route)  59.9 us
    dot_general x4, matrix products, refine_rows(): jnp.einsum('fh,xyhz->xyfz', weights_out, hidden, preferred_element_type=j...  45.2 us
    ppermute x12, starting transfers between devices, from_partner(): return lax.ppermute(block, axis, route)  19.3 us
    all_to_all x1, blocking collectives, body(): lax.all_to_all(stacked, 'section', split_axis=0, concat_axis=1, tiled=True)  13.8 us
    ppermute x8, starting transfers between devices, extended_2(): after = lax.ppermute(leading, axis, down)  10.6 us
    ppermute x8, starting transfers between devices, extended_2(): before = lax.ppermute(last, axis, up)  10.5 us
  transfers between devices with their start and end apart: 48, of which 30 were waited for; matrix products, arithmetic and copies ran while one was open for 16% of the time, Pallas kernels for 0%

profile of v1, /device:TPU:0, one launch (start us, length us, event | category | flops | bytes accessed | tf_op | source)
XLA Modules:
  0.0 500.0 jit_solution(15647424689351653370)
XLA Ops:
  7.8 2.2 all-gather
  9.9 2.9 collective-permute-start
  13.8 9.2 %collective-permute-done = bf16[8,80,2,128]{3,1,2,0:T(8,128)(2,1)} collective-permute-done((bf16[8,80,2,128]{3,1,2,0:T(8,128)(2,1)S(1)}, bf16[8,80,2,128]{3,1,2,0:T(8,128)(2,1)}, u32[]{:S(2)}, u32[]{:S(2)}) %collective-permute-start) | collective-permute-done | bytes 327712 | tf_op jit(solution)/shard_map/ppermute | solution.py:163
  23.7 10.5 %collective-permute-done.1 = bf16[8,80,2,128]{3,1,2,0:T(8,128)(2,1)} collective-permute-done((bf16[8,80,2,128]{3,1,2,0:T(8,128)(2,1)}, bf16[8,80,2,128]{3,1,2,0:T(8,128)(2,1)}, u32[]{:S(2)}, u32[]{:S(2)}) %collective-permute-start.1) | collective-permute-done | bytes 327712 | tf_op jit(solution)/shard_map/ppermute | solution.py:163
  34.9 9.7 %collective-permute-done.2 = bf16[8,80,2,128]{3,1,2,0:T(8,128)(2,1)S(1)} collective-permute-done((bf16[8,80,2,128]{3,1,2,0:T(8,128)(2,1)}, bf16[8,80,2,128]{3,1,2,0:T(8,128)(2,1)S(1)}, u32[]{:S(2)}, u32[]{:S(2)}) %collective-permute-start.2) | collective-permute-done | bytes 327712 | tf_op jit(solution)/shard_map/ppermute | solution.py:163
  47.4 2.2 collective-permute-start.3
  50.8 1.6 constant_dynamic-slice_fusion
  52.3 2.7 collective-permute-done.3
  56.4 1.8 collective-permute-start.4
  58.8 4.8 collective-permute-done.4
  72.6 8.2 %all-gather.1 = f32[4,1,128]{2,1,0:T(1,128)S(1)} all-gather(f32[1,1,128]{2,1,0:T(1,128)S(1)} %bitcast.672), channel_id=1, replica_groups=mesh['section'=4,'coil'=4,'cuts'=2] {'section'}, dimensions={0}, use_global_device_ids=true | all-gather | bytes 2560 | tf_op jit(solution)/shard_map/all_gather | solution.py:233
  81.3 8.2 %all_gather.26 = bf16[4,128,18]{1,2,0:T(8,128)(2,1)S(1)} all-gather(bf16[1,128,18]{1,2,0:T(8,128)(2,1)S(1)} %copy-done.29), channel_id=1, replica_groups=mesh['section'=4,'coil'=4,'cuts'=2] {'section'}, dimensions={0}, use_global_device_ids=true | all-gather | bytes 23040 | tf_op jit(solution)/shard_map/all_gather | solution.py:236
  89.5 8.9 %all-reduce.8 = f32[4]{0:T(128)S(1)} all-reduce(f32[4]{0:T(128)S(1)} %dynamic-update-slice), channel_id=1, replica_groups=mesh['section'=4,'coil'=4,'cuts'=2] {'section'}, use_global_device_ids=true, to_apply=%add.8 | all-reduce | flops 4 | bytes 32
  98.4 7.4 %all_gather.28 = bf16[4,18,128]{2,1,0:T(8,128)(2,1)S(1)} all-gather(bf16[1,18,128]{2,1,0:T(8,128)(2,1)S(1)} %copy-done.30), channel_id=1, replica_groups=mesh['section'=4,'coil'=4,'cuts'=2] {'section'}, dimensions={0}, use_global_device_ids=true | all-gather | bytes 23040 | tf_op jit(solution)/shard_map/all_gather | solution.py:237
  108.5 1.8 copy.298
  110.4 11.3 %fusion.22 = bf16[8,40,128,18]{2,3,1,0:T(8,128)(2,1)} fusion(f32[128]{0:T(128)S(1)} %get-tuple-element.76, bf16[8,40,18,128]{3,1,2,0:T(8,128)(2,1)} %bitcast.655, bf16[4,18,128]{2,1,0:T(8,128)(2,1)S(1)} %all_gather.28, bf16[4,128,18]{1,2,0:T(8,128)(2,1)S(1)} %all_gather.26), kind=kOutput, calls=%fused_computation.51 | convolution fusion | flops 408944640 | bytes 2961920 | tf_op jit(solution)/shard_map/fh,xyhz->xyfz/dot_general | solution.py:134
  121.7 1.7 copy.622
  127.8 1.5 collective-permute-start.5
  130.2 4.6 collective-permute-done.5
  136.0 2.0 all_gather.29
  138.0 11.6 %collective-permute-done.10 = bf16[8,80,2,128]{3,1,2,0:T(8,128)(2,1)S(1)} collective-permute-done((bf16[8,80,2,128]{3,1,2,0:T(8,128)(2,1)S(1)}, bf16[8,80,2,128]{3,1,2,0:T(8,128)(2,1)S(1)}, u32[]{:S(2)}, u32[]{:S(2)}) %collective-permute-start.10) | collective-permute-done | bytes 327712 | tf_op jit(solution)/shard_map/ppermute | solution.py:163
  149.6 10.7 %collective-permute-done.11 = bf16[8,80,2,128]{3,1,2,0:T(8,128)(2,1)S(1)} collective-permute-done((bf16[8,80,2,128]{3,1,2,0:T(8,128)(2,1)S(1)}, bf16[8,80,2,128]{3,1,2,0:T(8,128)(2,1)S(1)}, u32[]{:S(2)}, u32[]{:S(2)}) %collective-permute-start.11) | collective-permute-done | bytes 327712 | tf_op jit(solution)/shard_map/ppermute | solution.py:163
  160.5 9.8 %collective-permute-done.12 = bf16[8,80,2,128]{3,1,2,0:T(8,128)(2,1)S(1)} collective-permute-done((bf16[8,80,2,128]{3,1,2,0:T(8,128)(2,1)S(1)}, bf16[8,80,2,128]{3,1,2,0:T(8,128)(2,1)S(1)}, u32[]{:S(2)}, u32[]{:S(2)}) %collective-permute-start.12) | collective-permute-done | bytes 327712 | tf_op jit(solution)/shard_map/ppermute | solution.py:163
  173.3 1.5 collective-permute-start.13
  174.8 5.7 %collective-permute-done.13 = bf16[16,40,2,128]{3,1,0,2:T(8,128)(2,1)S(1)} collective-permute-done((bf16[16,40,2,128]{3,1,0,2:T(8,128)(2,1)S(1)}, bf16[16,40,2,128]{3,1,0,2:T(8,128)(2,1)S(1)}, u32[]{:S(2)}, u32[]{:S(2)}) %collective-permute-start.13) | collective-permute-done | bytes 327712 | tf_op jit(solution)/shard_map/ppermute | solution.py:28
  181.9 1.5 collective-permute-start.14
  183.4 5.6 %collective-permute-done.14 = bf16[16,40,2,128]{3,1,0,2:T(8,128)(2,1)S(1)} collective-permute-done((bf16[16,40,2,128]{3,1,0,2:T(8,128)(2,1)S(1)}, bf16[16,40,2,128]{3,1,0,2:T(8,128)(2,1)S(1)}, u32[]{:S(2)}, u32[]{:S(2)}) %collective-permute-start.14) | collective-permute-done | bytes 327712 | tf_op jit(solution)/shard_map/ppermute | solution.py:28
  196.0 1.8 collective-permute-done.17
  200.4 21.7 %reduce-scatter.13.cloned.1.call-done = bf16[8,80,2,128]{3,1,2,0:T(8,128)(2,1)} async-done(((bf16[32,80,2,128]{3,1,2,0:T(8,128)(2,1)}), bf16[8,80,2,128]{3,1,2,0:T(8,128)(2,1)}) %reduce-scatter.13.cloned.1.call-update) | async-done | bytes 327696 | tf_op jit(solution)/shard_map/reduce_scatter | solution.py:144
  222.1 1.8 copy.318
  224.4 11.3 %fusion.20 = bf16[8,40,128,18]{2,3,1,0:T(8,128)(2,1)} fusion(f32[128]{0:T(128)S(1)} %copy-done.33, bf16[8,40,18,128]{3,1,2,0:T(8,128)(2,1)} %bitcast.656, bf16[4,18,128]{2,1,0:T(8,128)(2,1)} %copy-done.24, bf16[4,128,18]{1,2,0:T(8,128)(2,1)S(1)} %all_gather.26), kind=kOutput, calls=%fused_computation.50 | convolution fusion | flops 408944640 | bytes 2961920 | tf_op jit(solution)/shard_map/fh,xyhz->xyfz/dot_general | solution.py:134
  235.7 1.7 copy.623
  241.3 1.5 collective-permute-start.15
  243.6 4.6 collective-permute-done.15
  249.5 2.0 all_gather.30
  251.5 11.6 %collective-permute-done.20 = bf16[8,80,2,128]{3,1,2,0:T(8,128)(2,1)S(1)} collective-permute-done((bf16[8,80,2,128]{3,1,2,0:T(8,128)(2,1)S(1)}, bf16[8,80,2,128]{3,1,2,0:T(8,128)(2,1)S(1)}, u32[]{:S(2)}, u32[]{:S(2)}) %collective-permute-start.20) | collective-permute-done | bytes 327712 | tf_op jit(solution)/shard_map/ppermute | solution.py:163
  263.1 10.7 %collective-permute-done.21 = bf16[8,80,2,128]{3,1,2,0:T(8,128)(2,1)S(1)} collective-permute-done((bf16[8,80,2,128]{3,1,2,0:T(8,128)(2,1)S(1)}, bf16[8,80,2,128]{3,1,2,0:T(8,128)(2,1)S(1)}, u32[]{:S(2)}, u32[]{:S(2)}) %collective-permute-start.21) | collective-permute-done | bytes 327712 | tf_op jit(solution)/shard_map/ppermute | solution.py:163
  273.9 9.8 %collective-permute-done.22 = bf16[8,80,2,128]{3,1,2,0:T(8,128)(2,1)S(1)} collective-permute-done((bf16[8,80,2,128]{3,1,2,0:T(8,128)(2,1)S(1)}, bf16[8,80,2,128]{3,1,2,0:T(8,128)(2,1)S(1)}, u32[]{:S(2)}, u32[]{:S(2)}) %collective-permute-start.22) | collective-permute-done | bytes 327712 | tf_op jit(solution)/shard_map/ppermute | solution.py:163
  286.5 1.5 collective-permute-start.23
  288.0 5.7 %collective-permute-done.23 = bf16[16,40,2,128]{3,1,0,2:T(8,128)(2,1)S(1)} collective-permute-done((bf16[16,40,2,128]{3,1,0,2:T(8,128)(2,1)S(1)}, bf16[16,40,2,128]{3,1,0,2:T(8,128)(2,1)S(1)}, u32[]{:S(2)}, u32[]{:S(2)}) %collective-permute-start.23) | collective-permute-done | bytes 327712 | tf_op jit(solution)/shard_map/ppermute | solution.py:28
  295.1 1.5 collective-permute-start.24
  296.7 5.6 %collective-permute-done.24 = bf16[16,40,2,128]{3,1,0,2:T(8,128)(2,1)S(1)} collective-permute-done((bf16[16,40,2,128]{3,1,0,2:T(8,128)(2,1)S(1)}, bf16[16,40,2,128]{3,1,0,2:T(8,128)(2,1)S(1)}, u32[]{:S(2)}, u32[]{:S(2)}) %collective-permute-start.24) | collective-permute-done | bytes 327712 | tf_op jit(solution)/shard_map/ppermute | solution.py:28
  309.2 1.8 collective-permute-done.27
  313.6 22.6 %reduce-scatter.17.cloned.1.call-done = bf16[8,80,2,128]{3,1,2,0:T(8,128)(2,1)} async-done(((bf16[32,80,2,128]{3,1,2,0:T(8,128)(2,1)}), bf16[8,80,2,128]{3,1,2,0:T(8,128)(2,1)}) %reduce-scatter.17.cloned.1.call-update) | async-done | bytes 327696 | tf_op jit(solution)/shard_map/reduce_scatter | solution.py:144
  336.2 1.8 copy.338
  338.3 11.3 %fusion.18 = bf16[8,40,128,18]{2,3,1,0:T(8,128)(2,1)} fusion(f32[128]{0:T(128)S(1)} %copy-done.32, bf16[8,40,18,128]{3,1,2,0:T(8,128)(2,1)} %bitcast.657, bf16[4,18,128]{2,1,0:T(8,128)(2,1)} %copy-done.24, bf16[4,128,18]{1,2,0:T(8,128)(2,1)S(1)} %all_gather.26), kind=kOutput, calls=%fused_computation.49 | convolution fusion | flops 408944640 | bytes 2961920 | tf_op jit(solution)/shard_map/fh,xyhz->xyfz/dot_general | solution.py:134
  349.6 1.7 copy.624
  355.1 1.5 collective-permute-start.25
  357.5 4.6 collective-permute-done.25
  363.4 2.0 all_gather.31
  365.5 11.6 %collective-permute-done.30 = bf16[8,80,2,128]{3,1,2,0:T(8,128)(2,1)S(1)} collective-permute-done((bf16[8,80,2,128]{3,1,2,0:T(8,128)(2,1)S(1)}, bf16[8,80,2,128]{3,1,2,0:T(8,128)(2,1)S(1)}, u32[]{:S(2)}, u32[]{:S(2)}) %collective-permute-start.30) | collective-permute-done | bytes 327712 | tf_op jit(solution)/shard_map/ppermute | solution.py:163
  377.0 10.7 %collective-permute-done.31 = bf16[8,80,2,128]{3,1,2,0:T(8,128)(2,1)S(1)} collective-permute-done((bf16[8,80,2,128]{3,1,2,0:T(8,128)(2,1)S(1)}, bf16[8,80,2,128]{3,1,2,0:T(8,128)(2,1)S(1)}, u32[]{:S(2)}, u32[]{:S(2)}) %collective-permute-start.31) | collective-permute-done | bytes 327712 | tf_op jit(solution)/shard_map/ppermute | solution.py:163
  387.9 9.8 %collective-permute-done.32 = bf16[8,80,2,128]{3,1,2,0:T(8,128)(2,1)S(1)} collective-permute-done((bf16[8,80,2,128]{3,1,2,0:T(8,128)(2,1)S(1)}, bf16[8,80,2,128]{3,1,2,0:T(8,128)(2,1)S(1)}, u32[]{:S(2)}, u32[]{:S(2)}) %collective-permute-start.32) | collective-permute-done | bytes 327712 | tf_op jit(solution)/shard_map/ppermute | solution.py:163
  402.2 5.7 %collective-permute-done.33 = bf16[16,40,2,128]{3,1,0,2:T(8,128)(2,1)S(1)} collective-permute-done((bf16[16,40,2,128]{3,1,0,2:T(8,128)(2,1)S(1)}, bf16[16,40,2,128]{3,1,0,2:T(8,128)(2,1)S(1)}, u32[]{:S(2)}, u32[]{:S(2)}) %collective-permute-start.33) | collective-permute-done | bytes 327712 | tf_op jit(solution)/shard_map/ppermute | solution.py:28
  409.3 1.5 collective-permute-start.34
  410.9 5.6 %collective-permute-done.34 = bf16[16,40,2,128]{3,1,0,2:T(8,128)(2,1)S(1)} collective-permute-done((bf16[16,40,2,128]{3,1,0,2:T(8,128)(2,1)S(1)}, bf16[16,40,2,128]{3,1,0,2:T(8,128)(2,1)S(1)}, u32[]{:S(2)}, u32[]{:S(2)}) %collective-permute-start.34) | collective-permute-done | bytes 327712 | tf_op jit(solution)/shard_map/ppermute | solution.py:28
  422.1 1.6 collective-permute-start.37
  427.8 22.6 %reduce-scatter.21.cloned.1.call-done = bf16[8,80,2,128]{3,1,2,0:T(8,128)(2,1)} async-done(((bf16[32,80,2,128]{3,1,2,0:T(8,128)(2,1)}), bf16[8,80,2,128]{3,1,2,0:T(8,128)(2,1)}) %reduce-scatter.21.cloned.1.call-update) | async-done | bytes 327696 | tf_op jit(solution)/shard_map/reduce_scatter | solution.py:144
  450.4 1.8 copy.358
  452.2 11.3 %fusion.16 = bf16[8,40,128,18]{2,3,1,0:T(8,128)(2,1)} fusion(f32[128]{0:T(128)S(1)} %get-tuple-element.79, bf16[8,40,18,128]{3,1,2,0:T(8,128)(2,1)} %bitcast.654, bf16[4,18,128]{2,1,0:T(8,128)(2,1)} %copy-done.24, bf16[4,128,18]{1,2,0:T(8,128)(2,1)S(1)} %all_gather.26), kind=kOutput, calls=%fused_computation.48 | convolution fusion | flops 408944640 | bytes 2961920 | tf_op jit(solution)/shard_map/fh,xyhz->xyfz/dot_general | solution.py:134
  463.5 1.7 copy.625
  469.1 1.6 collective-permute-start.35
  471.5 4.6 collective-permute-done.35
  477.9 13.8 %all_to_all.12 = bf16[4,1,8,40,2,128]{5,4,3,2,1,0:T(2,128)(2,1)S(1)} all-to-all(bf16[4,1,8,40,2,128]{5,4,3,2,1,0:T(2,128)(2,1)S(1)} %copy.365), channel_id=1, replica_groups=mesh['section'=4,'coil'=4,'cuts'=2] {'section'}, dimensions={0} | all-to-all | bytes 1310720 | tf_op jit(solution)/shard_map/all_to_all | solution.py:260
  (320 shorter events, 89.6 us)
Async XLA Ops:
  6.5 16.5 %copy-start = (bf16[2,1,32,80,2,128]{5,4,3,2,1,0:T(2,128)(2,1)S(1)}, bf16[2,1,32,80,2,128]{5,4,3,2,1,0:T(2,128)(2,1)}, u32[]{:S(2)}) copy-start(bf16[2,1,32,80,2,128]{5,4,3,2,1,0:T(2,128)(2,1)} %param.11) | copy-start | bytes 7864324
  6.5 101.9 %reduce-scatter.9.cloned.1.call-start = ((), (), s32[]{:S(2)}) async-start(), calls=%async_computation.9 | async-start | bytes 1638400 | tf_op jit(solution)/shard_map/reduce_scatter | solution.py:144
  9.9 13.1 %collective-permute-start = (bf16[8,80,2,128]{3,1,2,0:T(8,128)(2,1)S(1)}, bf16[8,80,2,128]{3,1,2,0:T(8,128)(2,1)}, u32[]{:S(2)}, u32[]{:S(2)}) collective-permute-start(bf16[8,80,2,128]{3,1,2,0:T(8,128)(2,1)S(1)} %bitcast.658), channel_id=1, source_target_pairs={{0,2},{2,4},{4,6},{6,0},{1,3},{3,5},{5,7},{7,1},{8,10},{10,12},{12... | collective-permute-start | bytes 983048 | tf_op jit(solution)/shard_map/ppermute | solution.py:163
  23.0 11.3 %collective-permute-start.1 = (bf16[8,80,2,128]{3,1,2,0:T(8,128)(2,1)}, bf16[8,80,2,128]{3,1,2,0:T(8,128)(2,1)}, u32[]{:S(2)}, u32[]{:S(2)}) collective-permute-start(bf16[8,80,2,128]{3,1,2,0:T(8,128)(2,1)} %collective-permute-done), channel_id=1, source_target_pairs={{0,2},{2,4},{4,6},{6,0},{1,3},{3,5},{5,7},{7,1},{8,10},{10,12},{12... | collective-permute-start | bytes 983048 | tf_op jit(solution)/shard_map/ppermute | solution.py:163
  34.3 10.3 %collective-permute-start.2 = (bf16[8,80,2,128]{3,1,2,0:T(8,128)(2,1)}, bf16[8,80,2,128]{3,1,2,0:T(8,128)(2,1)S(1)}, u32[]{:S(2)}, u32[]{:S(2)}) collective-permute-start(bf16[8,80,2,128]{3,1,2,0:T(8,128)(2,1)} %collective-permute-done.1), channel_id=1, source_target_pairs={{0,2},{2,4},{4,6},{6,0},{1,3},{3,5},{5,7},{7,1},{8,10},{10,12},{12... | collective-permute-start | bytes 983048 | tf_op jit(solution)/shard_map/ppermute | solution.py:163
  34.9 11.5 %copy-start.10 = (bf16[128,128]{1,0:T(8,128)(2,1)}, bf16[128,128]{1,0:T(8,128)(2,1)S(1)}, u32[]{:S(2)}) copy-start(bf16[128,128]{1,0:T(8,128)(2,1)S(1)} %get-tuple-element.92) | copy-start | bytes 98308
  47.4 7.7 %collective-permute-start.3 = (bf16[16,40,2,128]{3,1,0,2:T(8,128)(2,1)S(1)}, bf16[16,40,2,128]{3,1,0,2:T(8,128)(2,1)S(1)}, u32[]{:S(2)}, u32[]{:S(2)}) collective-permute-start(bf16[16,40,2,128]{3,1,0,2:T(8,128)(2,1)S(1)} %dynamic-slice_bitcast_fusion.7), channel_id=1, source_target_pairs={{0,8},{8,0},{16,24},{24,16},{1,9},{9,1},{17,25},{25,17},{2,10},{10... | collective-permute-start | bytes 983048 | tf_op jit(solution)/shard_map/ppermute | solution.py:28
  56.4 7.1 %collective-permute-start.4 = (bf16[16,40,2,128]{3,1,0,2:T(8,128)(2,1)S(1)}, bf16[16,40,2,128]{3,1,0,2:T(8,128)(2,1)S(1)}, u32[]{:S(2)}, u32[]{:S(2)}) collective-permute-start(bf16[16,40,2,128]{3,1,0,2:T(8,128)(2,1)S(1)} %dynamic-slice_bitcast_fusion.6), channel_id=1, source_target_pairs={{0,8},{8,0},{16,24},{24,16},{1,9},{9,1},{17,25},{25,17},{2,10},{10... | collective-permute-start | bytes 983048 | tf_op jit(solution)/shard_map/ppermute | solution.py:28
  66.6 14.7 %copy-start.29 = (bf16[1,128,18]{1,2,0:T(8,128)(2,1)S(1)}, bf16[1,128,18]{1,2,0:T(8,128)(2,1)}, u32[]{:S(2)}) copy-start(bf16[1,128,18]{1,2,0:T(8,128)(2,1)} %param.15) | copy-start | bytes 13828
  66.6 31.8 %copy-start.30 = (bf16[1,18,128]{2,1,0:T(8,128)(2,1)S(1)}, bf16[1,18,128]{2,1,0:T(8,128)(2,1)}, u32[]{:S(2)}) copy-start(bf16[1,18,128]{2,1,0:T(8,128)(2,1)} %param.17) | copy-start | bytes 13828
  67.9 58.9 %reduce-scatter.11.cloned.1.call-start = ((), (), s32[]{:S(2)}) async-start(), calls=%async_computation.10 | async-start | bytes 491520 | tf_op jit(solution)/shard_map/reduce_scatter | solution.py:150
  67.9 37.9 %collective-permute-start.6 = (bf16[8,1,2,128]{3,1,2,0:T(2,128)(2,1)S(1)}, bf16[8,1,2,128]{3,1,2,0:T(2,128)(2,1)S(1)}, u32[]{:S(2)}, u32[]{:S(2)}) collective-permute-start(bf16[8,1,2,128]{3,1,2,0:T(2,128)(2,1)S(1)} %get-tuple-element.70), channel_id=1, source_target_pairs={{0,1},{2,3},{4,5},{6,7},{8,9},{10,11},{12,13},{14,15},{16,17},{18,... | collective-permute-start | bytes 12296 | tf_op jit(solution)/shard_map/ppermute | solution.py:15
  69.2 36.6 %collective-permute-start.7 = (bf16[8,1,2,128]{3,1,2,0:T(2,128)(2,1)S(1)}, bf16[8,1,2,128]{3,1,2,0:T(2,128)(2,1)S(1)}, u32[]{:S(2)}, u32[]{:S(2)}) collective-permute-start(bf16[8,1,2,128]{3,1,2,0:T(2,128)(2,1)S(1)} %get-tuple-element.71), channel_id=1, source_target_pairs={{1,0},{3,2},{5,4},{7,6},{9,8},{11,10},{13,12},{15,14},{17,16},{19,... | collective-permute-start | bytes 12296 | tf_op jit(solution)/shard_map/ppermute | solution.py:16
  110.3 111.7 %reduce-scatter.13.cloned.1.call-start = ((), (), s32[]{:S(2)}) async-start(), calls=%async_computation.11 | async-start | bytes 1638400 | tf_op jit(solution)/shard_map/reduce_scatter | solution.py:144
  123.5 5.8 %collective-permute-start.8 = (bf16[8,1,18,128]{3,1,2,0:T(2,128)(2,1)S(1)}, bf16[8,1,18,128]{3,1,2,0:T(2,128)(2,1)S(1)}, u32[]{:S(2)}, u32[]{:S(2)}) collective-permute-start(bf16[8,1,18,128]{3,1,2,0:T(2,128)(2,1)S(1)} %get-tuple-element.20), channel_id=1, source_target_pairs={{0,1},{2,3},{4,5},{6,7},{8,9},{10,11},{12,13},{14,15},{16,17},{18,... | collective-permute-start | bytes 110600 | tf_op jit(solution)/shard_map/ppermute | solution.py:15
  124.8 4.5 collective-permute-start.9
  127.8 7.0 %copy-start.2 = (bf16[8,40,2,128]{3,0,2,1:T(8,128)(2,1)S(1)}, bf16[8,40,2,128]{3,0,2,1:T(8,128)(2,1)}, u32[]{:S(2)}) copy-start(bf16[8,40,2,128]{3,0,2,1:T(8,128)(2,1)} %reduce-scatter.11.cloned.1.call-done) | copy-start | bytes 491524
  127.8 7.0 %collective-permute-start.5 = (bf16[8,40,2,128]{3,1,2,0:T(8,128)(2,1)S(1)}, bf16[8,40,2,128]{3,1,2,0:T(8,128)(2,1)S(1)}, u32[]{:S(2)}, u32[]{:S(2)}) collective-permute-start(bf16[8,40,2,128]{3,1,2,0:T(8,128)(2,1)S(1)} %copy.299), channel_id=1, source_target_pairs={{0,8},{8,0},{16,24},{24,16},{1,9},{9,1},{17,25},{25,17},{2,10},{10... | collective-permute-start | bytes 491528 | tf_op jit(solution)/shard_map/ppermute | solution.py:28
  138.0 11.6 %collective-permute-start.10 = (bf16[8,80,2,128]{3,1,2,0:T(8,128)(2,1)S(1)}, bf16[8,80,2,128]{3,1,2,0:T(8,128)(2,1)S(1)}, u32[]{:S(2)}, u32[]{:S(2)}) collective-permute-start(bf16[8,80,2,128]{3,1,2,0:T(8,128)(2,1)S(1)} %all_gather.29), channel_id=1, source_target_pairs={{0,2},{2,4},{4,6},{6,0},{1,3},{3,5},{5,7},{7,1},{8,10},{10,12},{12... | collective-permute-start | bytes 983048 | tf_op jit(solution)/shard_map/ppermute | solution.py:163
  149.6 10.7 %collective-permute-start.11 = (bf16[8,80,2,128]{3,1,2,0:T(8,128)(2,1)S(1)}, bf16[8,80,2,128]{3,1,2,0:T(8,128)(2,1)S(1)}, u32[]{:S(2)}, u32[]{:S(2)}) collective-permute-start(bf16[8,80,2,128]{3,1,2,0:T(8,128)(2,1)S(1)} %collective-permute-done.10), channel_id=1, source_target_pairs={{0,2},{2,4},{4,6},{6,0},{1,3},{3,5},{5,7},{7,1},{8,10},{10,12},{12... | collective-permute-start | bytes 983048 | tf_op jit(solution)/shard_map/ppermute | solution.py:163
  160.3 10.1 %collective-permute-start.12 = (bf16[8,80,2,128]{3,1,2,0:T(8,128)(2,1)S(1)}, bf16[8,80,2,128]{3,1,2,0:T(8,128)(2,1)S(1)}, u32[]{:S(2)}, u32[]{:S(2)}) collective-permute-start(bf16[8,80,2,128]{3,1,2,0:T(8,128)(2,1)S(1)} %collective-permute-done.11), channel_id=1, source_target_pairs={{0,2},{2,4},{4,6},{6,0},{1,3},{3,5},{5,7},{7,1},{8,10},{10,12},{12... | collective-permute-start | bytes 983048 | tf_op jit(solution)/shard_map/ppermute | solution.py:163
  173.3 7.5 %copy-start.7 = (bf16[1,1,32,40,2,128]{5,4,3,2,1,0:T(2,128)(2,1)S(1)}, bf16[1,1,32,40,2,128]{5,4,3,2,1,0:T(2,128)(2,1)}, u32[]{:S(2)}) copy-start(bf16[1,1,32,40,2,128]{5,4,3,2,1,0:T(2,128)(2,1)} %copy-done.6) | copy-start | bytes 1966084
  173.3 7.5 %copy-start.14 = (bf16[2,32,2,32,1]{1,3,0,4,2:T(8,128)(2,1)S(1)}, bf16[2,32,2,32,1]{1,3,0,4,2:T(8,128)(2,1)}, u32[]{:S(2)}) copy-start(bf16[2,32,2,32,1]{1,3,0,4,2:T(8,128)(2,1)} %copy-done.13) | copy-start | bytes 24580
  173.3 7.5 %copy-start.26 = (f32[40,128]{1,0:T(8,128)S(1)}, f32[40,128]{1,0:T(8,128)}, u32[]{:S(2)}) copy-start(f32[40,128]{1,0:T(8,128)} %copy-done.25) | copy-start | bytes 61444
  173.3 7.2 %collective-permute-start.13 = (bf16[16,40,2,128]{3,1,0,2:T(8,128)(2,1)S(1)}, bf16[16,40,2,128]{3,1,0,2:T(8,128)(2,1)S(1)}, u32[]{:S(2)}, u32[]{:S(2)}) collective-permute-start(bf16[16,40,2,128]{3,1,0,2:T(8,128)(2,1)S(1)} %dynamic-slice_bitcast_fusion.5), channel_id=1, source_target_pairs={{0,8},{8,0},{16,24},{24,16},{1,9},{9,1},{17,25},{25,17},{2,10},{10... | collective-permute-start | bytes 983048 | tf_op jit(solution)/shard_map/ppermute | solution.py:28
  181.9 7.1 %collective-permute-start.14 = (bf16[16,40,2,128]{3,1,0,2:T(8,128)(2,1)S(1)}, bf16[16,40,2,128]{3,1,0,2:T(8,128)(2,1)S(1)}, u32[]{:S(2)}, u32[]{:S(2)}) collective-permute-start(bf16[16,40,2,128]{3,1,0,2:T(8,128)(2,1)S(1)} %dynamic-slice_bitcast_fusion.4), channel_id=1, source_target_pairs={{0,8},{8,0},{16,24},{24,16},{1,9},{9,1},{17,25},{25,17},{2,10},{10... | collective-permute-start | bytes 983048 | tf_op jit(solution)/shard_map/ppermute | solution.py:28
  193.3 47.0 %reduce-scatter.15.cloned.1.call-start = ((), (), s32[]{:S(2)}) async-start(), calls=%async_computation.12 | async-start | bytes 491520 | tf_op jit(solution)/shard_map/reduce_scatter | solution.py:150
  193.4 2.6 collective-permute-start.16
  194.7 3.1 collective-permute-start.17
  199.0 25.5 %copy-start.33 = (f32[128]{0:T(128)S(1)}, f32[128]{0:T(128)}, u32[]{:S(2)}) copy-start(f32[128]{0:T(128)} %get-tuple-element.78) | copy-start | bytes 1540
  223.9 112.3 %reduce-scatter.17.cloned.1.call-start = ((), (), s32[]{:S(2)}) async-start(), calls=%async_computation.13 | async-start | bytes 1638400 | tf_op jit(solution)/shard_map/reduce_scatter | solution.py:144
  237.6 5.2 %collective-permute-start.18 = (bf16[8,1,18,128]{3,1,2,0:T(2,128)(2,1)S(1)}, bf16[8,1,18,128]{3,1,2,0:T(2,128)(2,1)S(1)}, u32[]{:S(2)}, u32[]{:S(2)}) collective-permute-start(bf16[8,1,18,128]{3,1,2,0:T(2,128)(2,1)S(1)} %get-tuple-element.18), channel_id=1, source_target_pairs={{0,1},{2,3},{4,5},{6,7},{8,9},{10,11},{12,13},{14,15},{16,17},{18,... | collective-permute-start | bytes 110600 | tf_op jit(solution)/shard_map/ppermute | solution.py:15
  239.0 3.8 collective-permute-start.19
  241.3 7.0 %collective-permute-start.15 = (bf16[8,40,2,128]{3,1,2,0:T(8,128)(2,1)S(1)}, bf16[8,40,2,128]{3,1,2,0:T(8,128)(2,1)S(1)}, u32[]{:S(2)}, u32[]{:S(2)}) collective-permute-start(bf16[8,40,2,128]{3,1,2,0:T(8,128)(2,1)S(1)} %copy.319), channel_id=1, source_target_pairs={{0,8},{8,0},{16,24},{24,16},{1,9},{9,1},{17,25},{25,17},{2,10},{10... | collective-permute-start | bytes 491528 | tf_op jit(solution)/shard_map/ppermute | solution.py:28
  251.5 11.6 %collective-permute-start.20 = (bf16[8,80,2,128]{3,1,2,0:T(8,128)(2,1)S(1)}, bf16[8,80,2,128]{3,1,2,0:T(8,128)(2,1)S(1)}, u32[]{:S(2)}, u32[]{:S(2)}) collective-permute-start(bf16[8,80,2,128]{3,1,2,0:T(8,128)(2,1)S(1)} %all_gather.30), channel_id=1, source_target_pairs={{0,2},{2,4},{4,6},{6,0},{1,3},{3,5},{5,7},{7,1},{8,10},{10,12},{12... | collective-permute-start | bytes 983048 | tf_op jit(solution)/shard_map/ppermute | solution.py:163
  263.1 10.7 %collective-permute-start.21 = (bf16[8,80,2,128]{3,1,2,0:T(8,128)(2,1)S(1)}, bf16[8,80,2,128]{3,1,2,0:T(8,128)(2,1)S(1)}, u32[]{:S(2)}, u32[]{:S(2)}) collective-permute-start(bf16[8,80,2,128]{3,1,2,0:T(8,128)(2,1)S(1)} %collective-permute-done.20), channel_id=1, source_target_pairs={{0,2},{2,4},{4,6},{6,0},{1,3},{3,5},{5,7},{7,1},{8,10},{10,12},{12... | collective-permute-start | bytes 983048 | tf_op jit(solution)/shard_map/ppermute | solution.py:163
  273.8 10.0 %collective-permute-start.22 = (bf16[8,80,2,128]{3,1,2,0:T(8,128)(2,1)S(1)}, bf16[8,80,2,128]{3,1,2,0:T(8,128)(2,1)S(1)}, u32[]{:S(2)}, u32[]{:S(2)}) collective-permute-start(bf16[8,80,2,128]{3,1,2,0:T(8,128)(2,1)S(1)} %collective-permute-done.21), channel_id=1, source_target_pairs={{0,2},{2,4},{4,6},{6,0},{1,3},{3,5},{5,7},{7,1},{8,10},{10,12},{12... | collective-permute-start | bytes 983048 | tf_op jit(solution)/shard_map/ppermute | solution.py:163
  286.5 7.5 %copy-start.8 = (bf16[1,1,32,40,2,128]{5,4,3,2,1,0:T(2,128)(2,1)S(1)}, bf16[1,1,32,40,2,128]{5,4,3,2,1,0:T(2,128)(2,1)}, u32[]{:S(2)}) copy-start(bf16[1,1,32,40,2,128]{5,4,3,2,1,0:T(2,128)(2,1)} %copy-done.6) | copy-start | bytes 1966084
  286.5 7.5 %copy-start.27 = (f32[40,128]{1,0:T(8,128)S(1)}, f32[40,128]{1,0:T(8,128)}, u32[]{:S(2)}) copy-start(f32[40,128]{1,0:T(8,128)} %copy-done.25) | copy-start | bytes 61444
  286.5 7.3 %collective-permute-start.23 = (bf16[16,40,2,128]{3,1,0,2:T(8,128)(2,1)S(1)}, bf16[16,40,2,128]{3,1,0,2:T(8,128)(2,1)S(1)}, u32[]{:S(2)}, u32[]{:S(2)}) collective-permute-start(bf16[16,40,2,128]{3,1,0,2:T(8,128)(2,1)S(1)} %dynamic-slice_bitcast_fusion.3), channel_id=1, source_target_pairs={{0,8},{8,0},{16,24},{24,16},{1,9},{9,1},{17,25},{25,17},{2,10},{10... | collective-permute-start | bytes 983048 | tf_op jit(solution)/shard_map/ppermute | solution.py:28
  295.1 7.1 %collective-permute-start.24 = (bf16[16,40,2,128]{3,1,0,2:T(8,128)(2,1)S(1)}, bf16[16,40,2,128]{3,1,0,2:T(8,128)(2,1)S(1)}, u32[]{:S(2)}, u32[]{:S(2)}) collective-permute-start(bf16[16,40,2,128]{3,1,0,2:T(8,128)(2,1)S(1)} %dynamic-slice_bitcast_fusion.2), channel_id=1, source_target_pairs={{0,8},{8,0},{16,24},{24,16},{1,9},{9,1},{17,25},{25,17},{2,10},{10... | collective-permute-start | bytes 983048 | tf_op jit(solution)/shard_map/ppermute | solution.py:28
  306.5 47.6 %reduce-scatter.19.cloned.1.call-start = ((), (), s32[]{:S(2)}) async-start(), calls=%async_computation.14 | async-start | bytes 491520 | tf_op jit(solution)/shard_map/reduce_scatter | solution.py:150
  306.6 2.6 collective-permute-start.26
  307.9 3.1 collective-permute-start.27
  312.2 26.1 %copy-start.32 = (f32[128]{0:T(128)S(1)}, f32[128]{0:T(128)}, u32[]{:S(2)}) copy-start(f32[128]{0:T(128)} %get-tuple-element.77) | copy-start | bytes 1540
  338.1 112.3 %reduce-scatter.21.cloned.1.call-start = ((), (), s32[]{:S(2)}) async-start(), calls=%async_computation.15 | async-start | bytes 1638400 | tf_op jit(solution)/shard_map/reduce_scatter | solution.py:144
  351.5 5.2 %collective-permute-start.28 = (bf16[8,1,18,128]{3,1,2,0:T(2,128)(2,1)S(1)}, bf16[8,1,18,128]{3,1,2,0:T(2,128)(2,1)S(1)}, u32[]{:S(2)}, u32[]{:S(2)}) collective-permute-start(bf16[8,1,18,128]{3,1,2,0:T(2,128)(2,1)S(1)} %get-tuple-element.16), channel_id=1, source_target_pairs={{0,1},{2,3},{4,5},{6,7},{8,9},{10,11},{12,13},{14,15},{16,17},{18,... | collective-permute-start | bytes 110600 | tf_op jit(solution)/shard_map/ppermute | solution.py:15
  352.8 3.8 collective-permute-start.29
  355.1 7.0 %collective-permute-start.25 = (bf16[8,40,2,128]{3,1,2,0:T(8,128)(2,1)S(1)}, bf16[8,40,2,128]{3,1,2,0:T(8,128)(2,1)S(1)}, u32[]{:S(2)}, u32[]{:S(2)}) collective-permute-start(bf16[8,40,2,128]{3,1,2,0:T(8,128)(2,1)S(1)} %copy.339), channel_id=1, source_target_pairs={{0,8},{8,0},{16,24},{24,16},{1,9},{9,1},{17,25},{25,17},{2,10},{10... | collective-permute-start | bytes 491528 | tf_op jit(solution)/shard_map/ppermute | solution.py:28
  365.5 11.6 %collective-permute-start.30 = (bf16[8,80,2,128]{3,1,2,0:T(8,128)(2,1)S(1)}, bf16[8,80,2,128]{3,1,2,0:T(8,128)(2,1)S(1)}, u32[]{:S(2)}, u32[]{:S(2)}) collective-permute-start(bf16[8,80,2,128]{3,1,2,0:T(8,128)(2,1)S(1)} %all_gather.31), channel_id=1, source_target_pairs={{0,2},{2,4},{4,6},{6,0},{1,3},{3,5},{5,7},{7,1},{8,10},{10,12},{12... | collective-permute-start | bytes 983048 | tf_op jit(solution)/shard_map/ppermute | solution.py:163
  377.0 10.7 %collective-permute-start.31 = (bf16[8,80,2,128]{3,1,2,0:T(8,128)(2,1)S(1)}, bf16[8,80,2,128]{3,1,2,0:T(8,128)(2,1)S(1)}, u32[]{:S(2)}, u32[]{:S(2)}) collective-permute-start(bf16[8,80,2,128]{3,1,2,0:T(8,128)(2,1)S(1)} %collective-permute-done.30), channel_id=1, source_target_pairs={{0,2},{2,4},{4,6},{6,0},{1,3},{3,5},{5,7},{7,1},{8,10},{10,12},{12... | collective-permute-start | bytes 983048 | tf_op jit(solution)/shard_map/ppermute | solution.py:163
  387.7 10.1 %collective-permute-start.32 = (bf16[8,80,2,128]{3,1,2,0:T(8,128)(2,1)S(1)}, bf16[8,80,2,128]{3,1,2,0:T(8,128)(2,1)S(1)}, u32[]{:S(2)}, u32[]{:S(2)}) collective-permute-start(bf16[8,80,2,128]{3,1,2,0:T(8,128)(2,1)S(1)} %collective-permute-done.31), channel_id=1, source_target_pairs={{0,2},{2,4},{4,6},{6,0},{1,3},{3,5},{5,7},{7,1},{8,10},{10,12},{12... | collective-permute-start | bytes 983048 | tf_op jit(solution)/shard_map/ppermute | solution.py:163
  400.7 7.5 %copy-start.9 = (bf16[1,1,32,40,2,128]{5,4,3,2,1,0:T(2,128)(2,1)S(1)}, bf16[1,1,32,40,2,128]{5,4,3,2,1,0:T(2,128)(2,1)}, u32[]{:S(2)}) copy-start(bf16[1,1,32,40,2,128]{5,4,3,2,1,0:T(2,128)(2,1)} %copy-done.6) | copy-start | bytes 1966084
  400.7 7.5 %copy-start.15 = (bf16[2,32,2,32,1]{1,3,0,4,2:T(8,128)(2,1)S(1)}, bf16[2,32,2,32,1]{1,3,0,4,2:T(8,128)(2,1)}, u32[]{:S(2)}) copy-start(bf16[2,32,2,32,1]{1,3,0,4,2:T(8,128)(2,1)} %copy-done.13) | copy-start | bytes 24580
  400.7 7.5 %copy-start.28 = (f32[40,128]{1,0:T(8,128)S(1)}, f32[40,128]{1,0:T(8,128)}, u32[]{:S(2)}) copy-start(f32[40,128]{1,0:T(8,128)} %copy-done.25) | copy-start | bytes 61444
  400.7 7.3 %collective-permute-start.33 = (bf16[16,40,2,128]{3,1,0,2:T(8,128)(2,1)S(1)}, bf16[16,40,2,128]{3,1,0,2:T(8,128)(2,1)S(1)}, u32[]{:S(2)}, u32[]{:S(2)}) collective-permute-start(bf16[16,40,2,128]{3,1,0,2:T(8,128)(2,1)S(1)} %dynamic-slice_bitcast_fusion.1), channel_id=1, source_target_pairs={{0,8},{8,0},{16,24},{24,16},{1,9},{9,1},{17,25},{25,17},{2,10},{10... | collective-permute-start | bytes 983048 | tf_op jit(solution)/shard_map/ppermute | solution.py:28
  409.3 7.1 %collective-permute-start.34 = (bf16[16,40,2,128]{3,1,0,2:T(8,128)(2,1)S(1)}, bf16[16,40,2,128]{3,1,0,2:T(8,128)(2,1)S(1)}, u32[]{:S(2)}, u32[]{:S(2)}) collective-permute-start(bf16[16,40,2,128]{3,1,0,2:T(8,128)(2,1)S(1)} %dynamic-slice_bitcast_fusion), channel_id=1, source_target_pairs={{0,8},{8,0},{16,24},{24,16},{1,9},{9,1},{17,25},{25,17},{2,10},{10... | collective-permute-start | bytes 983048 | tf_op jit(solution)/shard_map/ppermute | solution.py:28
  420.8 47.3 %reduce-scatter.23.cloned.1.call-start = ((), (), s32[]{:S(2)}) async-start(), calls=%async_computation.16 | async-start | bytes 491520 | tf_op jit(solution)/shard_map/reduce_scatter | solution.py:150
  420.8 2.9 collective-permute-start.36
  422.1 3.1 collective-permute-start.37
  465.4 5.2 %collective-permute-start.38 = (bf16[8,1,18,128]{3,1,2,0:T(2,128)(2,1)S(1)}, bf16[8,1,18,128]{3,1,2,0:T(2,128)(2,1)S(1)}, u32[]{:S(2)}, u32[]{:S(2)}) collective-permute-start(bf16[8,1,18,128]{3,1,2,0:T(2,128)(2,1)S(1)} %get-tuple-element.14), channel_id=1, source_target_pairs={{0,1},{2,3},{4,5},{6,7},{8,9},{10,11},{12,13},{14,15},{16,17},{18,... | collective-permute-start | bytes 110600 | tf_op jit(solution)/shard_map/ppermute | solution.py:15
  466.8 3.9 collective-permute-start.39
  469.1 7.0 %collective-permute-start.35 = (bf16[8,40,2,128]{3,1,2,0:T(8,128)(2,1)S(1)}, bf16[8,40,2,128]{3,1,2,0:T(8,128)(2,1)S(1)}, u32[]{:S(2)}, u32[]{:S(2)}) collective-permute-start(bf16[8,40,2,128]{3,1,2,0:T(8,128)(2,1)S(1)} %copy.359), channel_id=1, source_target_pairs={{0,8},{8,0},{16,24},{24,16},{1,9},{9,1},{17,25},{25,17},{2,10},{10... | collective-permute-start | bytes 491528 | tf_op jit(solution)/shard_map/ppermute | solution.py:28
  477.3 15.4 %copy-start.1 = (bf16[2,1,32,80,2,128]{5,4,3,2,1,0:T(2,128)(2,1)S(1)}, bf16[2,1,32,80,2,128]{5,4,3,2,1,0:T(2,128)(2,1)}, u32[]{:S(2)}) copy-start(bf16[2,1,32,80,2,128]{5,4,3,2,1,0:T(2,128)(2,1)} %param.11) | copy-start | bytes 7864324
  (19 other events, 69.3 us)
Sparse Core Ops, SparseCore 0:
  68.0 29.8 reduce-scatter.8
  110.4 4.9 reduce-scatter.10
  193.4 28.5 reduce-scatter.12
  224.1 6.4 reduce-scatter.14
  306.7 29.4 reduce-scatter.16
  338.3 6.4 reduce-scatter.18
  420.9 29.4 reduce-scatter.20
  452.6 6.4 reduce-scatter.22
